TPU v7x, 256 devices: a whole 4x4x8 slice. The times are simulated.
256 devices in a mesh: segment: 8 (over x_lo, y), lat: 16 (over z, x_hi), dp: 2 (over core).
Axes of the slice: x: 4 (x_hi: 2, x_lo: 2; x = x_hi * 2 + x_lo), y: 4, z: 8, core: 2. Of those that a mesh axis runs over, the one named last changes fastest.
Arguments:
- initial: bfloat16 [8, 192, 32, 128], P('dp', None, 'lat'), may hold values from -6 to 6
- kernel: bfloat16 [8, 192, 9, 192], P('segment'), may hold values from -0.078125 to 0.078125
- bias: float32 [8, 192], P('segment'), may hold values from -0.6 to 0.6
- cotangent: bfloat16 [2, 8, 192, 32, 128], P(None, 'dp', None, 'lat'), may hold values from -6 to 6
Outputs:
- section_out: bfloat16 [8, 8, 192, 32, 128], P('segment', 'dp', None, 'lat')
- state_adjoint: float32 [8, 8, 192, 32, 128], P('segment', 'dp', None, 'lat')
- kernel_grad: float32 [8, 192, 9, 192], P('segment')
- bias_grad: float32 [8, 192], P('segment')
All inputs are finite; a program needn't handle non-finite values.
Results may differ from a plain program's by a relative error of at most 0.028.
Values may be sent and summed in bfloat16 or wider, within the bound.
A program may use at most 64 MiB of HBM per device.

v0:
```python
import math

import jax
import jax.numpy as jnp
from jax import lax
from jax.sharding import PartitionSpec as P

STEPS = 2


def passed_along(value, axis, steps):
    count = lax.axis_size(axis)
    pairs = [(source, (source + steps) % count) for source in range(count)]
    return lax.ppermute(value, axis, pairs)


def padded_2(block, sides, width):
    for axis, dim in sides:
        count = lax.axis_size(axis)
        forward = [(i, i + 1) for i in range(count - 1)]
        backward = [(target, source) for source, target in forward]
        low = lax.ppermute(
            lax.slice_in_dim(block, block.shape[dim] - width, None, axis=dim), axis, forward
        )
        high = lax.ppermute(lax.slice_in_dim(block, 0, width, axis=dim), axis, backward)
        block = jnp.concatenate([low, block, high], axis=dim)
    return block


def silu_value(values):
    return values / (1.0 + jnp.exp(-values))


def silu_slope(values):
    sigmoid_v = 1.0 / (1.0 + jnp.exp(-values))
    return sigmoid_v * (1.0 + values * (1.0 - sigmoid_v))


def tap_columns(padded):
    band_rows = padded.shape[1] - 2
    pieces = []
    for row_tap in range(3):
        strip = padded[:, row_tap : row_tap + band_rows, :]
        for col_tap in range(3):
            pieces.append(jnp.roll(strip, 1 - col_tap, axis=2))
    stacked = jnp.stack(pieces, axis=0)
    return stacked.reshape(9 * padded.shape[0], band_rows * padded.shape[2])


def back_columns(padded):
    band_rows = padded.shape[1] - 2
    pieces = []
    for row_tap in range(3):
        strip = padded[:, 2 - row_tap : 2 - row_tap + band_rows, :]
        for col_tap in range(3):
            pieces.append(jnp.roll(strip, col_tap - 1, axis=2))
    stacked = jnp.stack(pieces, axis=0)
    return stacked.reshape(9, padded.shape[0], band_rows * padded.shape[2])


def take_slot(buffer, slot):
    return lax.dynamic_index_in_dim(buffer, slot, 0, keepdims=False)


def put_slot(buffer, slot, value, flag):
    previous = lax.dynamic_index_in_dim(buffer, slot, 0, keepdims=False)
    return lax.dynamic_update_index_in_dim(buffer, jnp.where(flag, value, previous), slot, 0)


def per_device(initial, kernel, bias, cotangent):
    segment_count = lax.axis_size("segment")
    position = lax.axis_index("segment")
    before = jnp.mod(position - 1, segment_count)
    after = jnp.mod(position + 1, segment_count)
    micro = initial.shape[0]
    channels = initial.shape[1]
    band_rows = initial.shape[2]
    longitude = initial.shape[3]
    band_shape = (channels, band_rows, longitude)
    applications = STEPS * segment_count
    flat_kernel = kernel[0].reshape(channels, 9 * channels)
    kernel_taps = kernel[0]
    offsets = bias[0][:, None, None]
    cot_flat = cotangent.reshape((STEPS * micro,) + band_shape)
    tick_count = STEPS * (segment_count + micro - 1)

    def plan(moment, where_at):
        phase_span = segment_count + micro - 1
        rollout_step = jnp.floor_divide(moment, phase_span)
        sample = moment - rollout_step * phase_span - where_at
        applied = rollout_step * segment_count + where_at
        active = (moment >= 0) & (rollout_step < STEPS) & (sample >= 0) & (sample < micro)
        return (jnp.clip(sample, 0, micro - 1), applied, active)

    zero_band = jnp.zeros(band_shape, jnp.bfloat16)
    acts_store = jnp.zeros((STEPS * micro, channels, band_rows + 2, longitude), jnp.bfloat16)

    def forward_tick(moment, carry):
        outgoing, arrived, saved_states, acts_kept, last_outputs = carry
        received = passed_along(outgoing, "segment", 1)
        sent_sample, sent_applied, sent_active = plan(moment - 1, before)
        arrived = put_slot(
            arrived, sent_sample, received, sent_active & (sent_applied < applications - 1)
        )
        sample, applied, active = plan(moment, position)
        current = jnp.where(applied == 0, take_slot(initial, sample), take_slot(arrived, sample))
        activated = silu_value(current.astype(jnp.float32)).astype(jnp.bfloat16)
        padded = padded_2(activated, (("lat", 1),), 1)

        def advance(unused):
            branch = jnp.dot(
                flat_kernel, tap_columns(padded), preferred_element_type=jnp.float32
            ).reshape(band_shape)
            return (current.astype(jnp.float32) + branch + offsets).astype(jnp.bfloat16)

        def holding(unused):
            return current

        produced = lax.cond(active, advance, holding, 0)
        slot = jnp.clip(applied // segment_count, 0, STEPS - 1) * micro + sample
        saved_states = put_slot(saved_states, slot, current, active)
        acts_kept = put_slot(acts_kept, slot, padded, active)
        last_outputs = put_slot(
            last_outputs, sample, produced, active & (applied >= applications - segment_count)
        )
        return (produced, arrived, saved_states, acts_kept, last_outputs)

    forward_start = (
        zero_band,
        jnp.zeros((micro,) + band_shape, jnp.bfloat16),
        jnp.zeros((STEPS * micro,) + band_shape, jnp.bfloat16),
        acts_store,
        jnp.zeros((micro,) + band_shape, jnp.bfloat16),
    )
    unused_out, unused_arrived, saved_states, acts_kept, last_outputs = lax.fori_loop(
        0, tick_count, forward_tick, forward_start
    )

    def backward_tick(turn, carry):
        outgoing, arrived, adjoints, kernel_sum, bias_sum = carry
        received = passed_along(outgoing, "segment", -1)
        sent_sample, sent_applied, sent_active = plan(tick_count - turn, after)
        arrived = put_slot(arrived, sent_sample, received, sent_active & (sent_applied >= 1))
        sample, applied, active = plan(tick_count - 1 - turn, position)
        incoming = jnp.where(
            applied == applications - 1,
            take_slot(cot_flat, (STEPS - 1) * micro + sample),
            take_slot(arrived, sample),
        )
        incoming_padded = padded_2(incoming, (("lat", 1),), 1)
        slot = jnp.clip(applied // segment_count, 0, STEPS - 1) * micro + sample
        current = take_slot(saved_states, slot)
        padded = take_slot(acts_kept, slot)
        step_end = (applied >= segment_count) & (jnp.mod(applied, segment_count) == 0)
        cot_slot = jnp.clip(applied // segment_count - 1, 0, STEPS - 1) * micro + sample

        def retreat(unused):
            gradient_rows = incoming.reshape(channels, band_rows * longitude)
            kernel_term = lax.dot_general(
                gradient_rows,
                tap_columns(padded),
                (((1,), (1,)), ((), ())),
                preferred_element_type=jnp.float32,
            )
            bias_term = jnp.sum(incoming.astype(jnp.float32), axis=(1, 2))
            transposed = lax.dot_general(
                kernel_taps,
                back_columns(incoming_padded),
                (((0, 1), (1, 0)), ((), ())),
                preferred_element_type=jnp.float32,
            ).reshape(band_shape)
            adjoint_here = (
                incoming.astype(jnp.float32) + silu_slope(current.astype(jnp.float32)) * transposed
            )
            adjoint_here = adjoint_here + jnp.where(
                step_end, take_slot(cot_flat, cot_slot).astype(jnp.float32), 0.0
            )
            return (kernel_sum + kernel_term, bias_sum + bias_term, adjoint_here)

        def resting(unused):
            return (kernel_sum, bias_sum, jnp.zeros(band_shape, jnp.float32))

        kernel_sum, bias_sum, adjoint_here = lax.cond(active, retreat, resting, 0)
        adjoints = put_slot(adjoints, sample, adjoint_here, active & (applied < segment_count))
        return (adjoint_here.astype(jnp.bfloat16), arrived, adjoints, kernel_sum, bias_sum)

    backward_start = (
        zero_band,
        jnp.zeros((micro,) + band_shape, jnp.bfloat16),
        jnp.zeros((micro,) + band_shape, jnp.float32),
        jnp.zeros((channels, 9 * channels), jnp.float32),
        jnp.zeros((channels,), jnp.float32),
    )
    unused_grad, unused_inbox, adjoints, kernel_sum, bias_sum = lax.fori_loop(
        0, tick_count, backward_tick, backward_start
    )
    kernel_total, bias_total = (
        lax.psum(kernel_sum.astype(jnp.bfloat16), ("lat", "dp")).astype(jnp.float32),
        lax.psum(bias_sum.astype(jnp.bfloat16), ("lat", "dp")).astype(jnp.float32),
    )
    normalizer = 1.0 / math.sqrt(
        micro * lax.axis_size("dp") * band_rows * lax.axis_size("lat") * longitude
    )
    kernel_grad = (kernel_total * normalizer).reshape(1, channels, 9, channels)
    bias_grad = (bias_total * normalizer)[None]
    return (last_outputs[None], adjoints[None], kernel_grad, bias_grad)


def solution(mesh):
    return jax.shard_map(
        per_device,
        mesh=mesh,
        in_specs=(
            P("dp", None, "lat", None),
            P("segment", None, None, None),
            P("segment", None),
            P(None, "dp", None, "lat", None),
        ),
        out_specs=(
            P("segment", "dp", None, "lat", None),
            P("segment", "dp", None, "lat", None),
            P("segment", None, None, None),
            P("segment", None),
        ),
        check_vma=False,
    )
```

profile of v0, /device:TPU:1, one launch (start us, length us, event | category | flops | bytes accessed | tf_op | source)
XLA Modules:
  0.0 2028.6 jit_solution(11901487231347078123)
XLA Ops:
  13.8 457.1 %while.48 = (s32[]{:T(128)}, bf16[192,2,128]{2,1,0:T(2,128)(2,1)}, bf16[4,192,2,128]{3,1,2,0:T(8,128)(2,1)S(1)}, bf16[8,192,2,128]{3,2,1,0:T(2,128)(2,1)}, bf16[...) while((s32[]{:T(128)}, bf16[192,2,128]{2,1,0:T(2,128)(2,1)}, ...), condition=%wide.region_3.4_spmd, body=%wide.region_0.3_spmd.sunk | while | flops 172425280 | bytes 14624630 | solution.py:135
  65.1 6.7 collective-permute-start.2
  87.1 6.7 collective-permute-start.2
  109.2 6.7 collective-permute-start.2
  126.9 6.7 collective-permute-start.2
  144.7 7.1 collective-permute-start.2
  181.6 7.6 collective-permute-start.2
  202.6 7.0 collective-permute-start.2
  223.0 7.0 collective-permute-start.2
  243.9 7.3 collective-permute-start.2
  290.0 6.7 collective-permute-start.2
  335.9 8.0 collective-permute-start.2
  356.0 8.5 collective-permute-start.2
  375.7 7.0 collective-permute-start.2
  394.2 7.6 collective-permute-start.2
  413.5 9.4 collective-permute-start.2
  436.2 8.8 collective-permute-start.2
  451.3 7.5 collective-permute-done
  460.3 7.7 collective-permute-start.2
  473.9 1163.2 %while.49 = (s32[]{:T(128)}, bf16[192,2,128]{2,1,0:T(2,128)(2,1)}, bf16[4,192,2,128]{3,2,1,0:T(2,128)(2,1)}, f32[4,192,2,128]{3,2,1,0:T(2,128)}, f32[192,1728]{1...) while((s32[]{:T(128)}, bf16[192,2,128]{2,1,0:T(2,128)(2,1)}, ...), condition=%wide.region_8.9_spmd, body=%wide.region_4.8_spmd.sunk | while | flops 343953472 | bytes 20231204 | solution.py:194
  474.1 8.7 collective-permute-start.3
  487.9 9.8 collective-permute-start.5
  503.0 35.6 %collective-permute-start.3 = (bf16[192,2,128]{2,1,0:T(2,128)(2,1)}, bf16[192,2,128]{2,1,0:T(2,128)(2,1)S(1)}, u32[]{:S(2)}, u32[]{:S(2)}) collective-permute-start(bf16[192,2,128]{2,1,0:T(2,128)(2,1)} %get-tuple-element.1480), channel_id=1, source_target_pairs={{0,224},{32,0},{64,32},{96,64},{128,96},{160,128},{192,160},{224,1... | collective-permute-start | bytes 294920 | tf_op jit(solution)/shard_map/while/body/eval_jaxpr/ppermute | solution.py:14
  543.9 7.1 collective-permute-start.5
  556.0 35.6 %collective-permute-start.3 = (bf16[192,2,128]{2,1,0:T(2,128)(2,1)}, bf16[192,2,128]{2,1,0:T(2,128)(2,1)S(1)}, u32[]{:S(2)}, u32[]{:S(2)}) collective-permute-start(bf16[192,2,128]{2,1,0:T(2,128)(2,1)} %get-tuple-element.1480), channel_id=1, source_target_pairs={{0,224},{32,0},{64,32},{96,64},{128,96},{160,128},{192,160},{224,1... | collective-permute-start | bytes 294920 | tf_op jit(solution)/shard_map/while/body/eval_jaxpr/ppermute | solution.py:14
  596.9 7.5 collective-permute-start.5
  610.4 34.1 %collective-permute-start.3 = (bf16[192,2,128]{2,1,0:T(2,128)(2,1)}, bf16[192,2,128]{2,1,0:T(2,128)(2,1)S(1)}, u32[]{:S(2)}, u32[]{:S(2)}) collective-permute-start(bf16[192,2,128]{2,1,0:T(2,128)(2,1)} %get-tuple-element.1480), channel_id=1, source_target_pairs={{0,224},{32,0},{64,32},{96,64},{128,96},{160,128},{192,160},{224,1... | collective-permute-start | bytes 294920 | tf_op jit(solution)/shard_map/while/body/eval_jaxpr/ppermute | solution.py:14
  649.8 8.8 collective-permute-start.5
  663.7 35.0 %collective-permute-start.3 = (bf16[192,2,128]{2,1,0:T(2,128)(2,1)}, bf16[192,2,128]{2,1,0:T(2,128)(2,1)S(1)}, u32[]{:S(2)}, u32[]{:S(2)}) collective-permute-start(bf16[192,2,128]{2,1,0:T(2,128)(2,1)} %get-tuple-element.1480), channel_id=1, source_target_pairs={{0,224},{32,0},{64,32},{96,64},{128,96},{160,128},{192,160},{224,1... | collective-permute-start | bytes 294920 | tf_op jit(solution)/shard_map/while/body/eval_jaxpr/ppermute | solution.py:14
  704.1 10.6 collective-permute-start.5
  729.4 7.4 collective-permute-start.5
  742.5 29.1 %collective-permute-start.3 = (bf16[192,2,128]{2,1,0:T(2,128)(2,1)}, bf16[192,2,128]{2,1,0:T(2,128)(2,1)S(1)}, u32[]{:S(2)}, u32[]{:S(2)}) collective-permute-start(bf16[192,2,128]{2,1,0:T(2,128)(2,1)} %get-tuple-element.1480), channel_id=1, source_target_pairs={{0,224},{32,0},{64,32},{96,64},{128,96},{160,128},{192,160},{224,1... | collective-permute-start | bytes 294920 | tf_op jit(solution)/shard_map/while/body/eval_jaxpr/ppermute | solution.py:14
  777.2 6.9 collective-permute-start.5
  793.4 52.0 %collective-permute-done.3 = bf16[192,2,128]{2,1,0:T(2,128)(2,1)S(1)} collective-permute-done((bf16[192,2,128]{2,1,0:T(2,128)(2,1)}, bf16[192,2,128]{2,1,0:T(2,128)(2,1)S(1)}, u32[]{:S(2)}, u32[]{:S(2)}) %collective-permute-start.3) | collective-permute-done | bytes 98336 | tf_op jit(solution)/shard_map/while/body/eval_jaxpr/ppermute | solution.py:14
  848.6 9.8 collective-permute-start.5
  860.4 33.2 %conditional.5 = (f32[192,1728]{1,0:T(8,128)S(1)}, f32[192]{0:T(256)S(1)}, f32[192,2,128]{2,1,0:T(2,128)}, bf16[192,2,128]{2,1,0:T(2,128)(2,1)}) conditional(s32[]{:T(128)} %convert_element_type.170, (f32[192,1728]{1,0:T(8,128)S(1)}, f32[192]{0:T(256)S(1)}) %tuple.180, (s32[]{:T(128)}, s32[]{:T(128)}, pred[]{:T(512)}, pred[]{:T(512)}, ...), branch_computations={%region_5.5_spmd, %region_6.7_spmd.clone} | conditional | flops 343216128 | bytes 17083920 | solution.py:183
  896.3 10.6 collective-permute-done.3
  919.5 33.2 %conditional.5 = (f32[192,1728]{1,0:T(8,128)S(1)}, f32[192]{0:T(256)S(1)}, f32[192,2,128]{2,1,0:T(2,128)}, bf16[192,2,128]{2,1,0:T(2,128)(2,1)}) conditional(s32[]{:T(128)} %convert_element_type.170, (f32[192,1728]{1,0:T(8,128)S(1)}, f32[192]{0:T(256)S(1)}) %tuple.180, (s32[]{:T(128)}, s32[]{:T(128)}, pred[]{:T(512)}, pred[]{:T(512)}, ...), branch_computations={%region_5.5_spmd, %region_6.7_spmd.clone} | conditional | flops 343216128 | bytes 17083920 | solution.py:183
  973.2 33.2 %conditional.5 = (f32[192,1728]{1,0:T(8,128)S(1)}, f32[192]{0:T(256)S(1)}, f32[192,2,128]{2,1,0:T(2,128)}, bf16[192,2,128]{2,1,0:T(2,128)(2,1)}) conditional(s32[]{:T(128)} %convert_element_type.170, (f32[192,1728]{1,0:T(8,128)S(1)}, f32[192]{0:T(256)S(1)}) %tuple.180, (s32[]{:T(128)}, s32[]{:T(128)}, pred[]{:T(512)}, pred[]{:T(512)}, ...), branch_computations={%region_5.5_spmd, %region_6.7_spmd.clone} | conditional | flops 343216128 | bytes 17083920 | solution.py:183
  1025.6 33.2 %conditional.5 = (f32[192,1728]{1,0:T(8,128)S(1)}, f32[192]{0:T(256)S(1)}, f32[192,2,128]{2,1,0:T(2,128)}, bf16[192,2,128]{2,1,0:T(2,128)(2,1)}) conditional(s32[]{:T(128)} %convert_element_type.170, (f32[192,1728]{1,0:T(8,128)S(1)}, f32[192]{0:T(256)S(1)}) %tuple.180, (s32[]{:T(128)}, s32[]{:T(128)}, pred[]{:T(512)}, pred[]{:T(512)}, ...), branch_computations={%region_5.5_spmd, %region_6.7_spmd.clone} | conditional | flops 343216128 | bytes 17083920 | solution.py:183
  1067.4 10.5 collective-permute-start.5
  1084.0 33.4 %collective-permute-start.3 = (bf16[192,2,128]{2,1,0:T(2,128)(2,1)}, bf16[192,2,128]{2,1,0:T(2,128)(2,1)S(1)}, u32[]{:S(2)}, u32[]{:S(2)}) collective-permute-start(bf16[192,2,128]{2,1,0:T(2,128)(2,1)} %get-tuple-element.1480), channel_id=1, source_target_pairs={{0,224},{32,0},{64,32},{96,64},{128,96},{160,128},{192,160},{224,1... | collective-permute-start | bytes 294920 | tf_op jit(solution)/shard_map/while/body/eval_jaxpr/ppermute | solution.py:14
  1122.6 7.7 collective-permute-start.5
  1136.4 34.4 %collective-permute-start.3 = (bf16[192,2,128]{2,1,0:T(2,128)(2,1)}, bf16[192,2,128]{2,1,0:T(2,128)(2,1)S(1)}, u32[]{:S(2)}, u32[]{:S(2)}) collective-permute-start(bf16[192,2,128]{2,1,0:T(2,128)(2,1)} %get-tuple-element.1480), channel_id=1, source_target_pairs={{0,224},{32,0},{64,32},{96,64},{128,96},{160,128},{192,160},{224,1... | collective-permute-start | bytes 294920 | tf_op jit(solution)/shard_map/while/body/eval_jaxpr/ppermute | solution.py:14
  1176.0 7.1 collective-permute-start.5
  1189.2 35.1 %collective-permute-start.3 = (bf16[192,2,128]{2,1,0:T(2,128)(2,1)}, bf16[192,2,128]{2,1,0:T(2,128)(2,1)S(1)}, u32[]{:S(2)}, u32[]{:S(2)}) collective-permute-start(bf16[192,2,128]{2,1,0:T(2,128)(2,1)} %get-tuple-element.1480), channel_id=1, source_target_pairs={{0,224},{32,0},{64,32},{96,64},{128,96},{160,128},{192,160},{224,1... | collective-permute-start | bytes 294920 | tf_op jit(solution)/shard_map/while/body/eval_jaxpr/ppermute | solution.py:14
  1229.5 7.8 collective-permute-start.5
  1242.4 35.4 %collective-permute-start.3 = (bf16[192,2,128]{2,1,0:T(2,128)(2,1)}, bf16[192,2,128]{2,1,0:T(2,128)(2,1)S(1)}, u32[]{:S(2)}, u32[]{:S(2)}) collective-permute-start(bf16[192,2,128]{2,1,0:T(2,128)(2,1)} %get-tuple-element.1480), channel_id=1, source_target_pairs={{0,224},{32,0},{64,32},{96,64},{128,96},{160,128},{192,160},{224,1... | collective-permute-start | bytes 294920 | tf_op jit(solution)/shard_map/while/body/eval_jaxpr/ppermute | solution.py:14
  1283.0 7.1 collective-permute-start.5
  1303.6 9.1 collective-permute-start.5
  1319.8 27.5 %collective-permute-start.3 = (bf16[192,2,128]{2,1,0:T(2,128)(2,1)}, bf16[192,2,128]{2,1,0:T(2,128)(2,1)S(1)}, u32[]{:S(2)}, u32[]{:S(2)}) collective-permute-start(bf16[192,2,128]{2,1,0:T(2,128)(2,1)} %get-tuple-element.1480), channel_id=1, source_target_pairs={{0,224},{32,0},{64,32},{96,64},{128,96},{160,128},{192,160},{224,1... | collective-permute-start | bytes 294920 | tf_op jit(solution)/shard_map/while/body/eval_jaxpr/ppermute | solution.py:14
  1352.5 7.1 collective-permute-start.5
  1368.9 54.3 %collective-permute-done.3 = bf16[192,2,128]{2,1,0:T(2,128)(2,1)S(1)} collective-permute-done((bf16[192,2,128]{2,1,0:T(2,128)(2,1)}, bf16[192,2,128]{2,1,0:T(2,128)(2,1)S(1)}, u32[]{:S(2)}, u32[]{:S(2)}) %collective-permute-start.3) | collective-permute-done | bytes 98336 | tf_op jit(solution)/shard_map/while/body/eval_jaxpr/ppermute | solution.py:14
  1426.4 9.2 collective-permute-start.5
  1437.5 33.2 %conditional.5 = (f32[192,1728]{1,0:T(8,128)S(1)}, f32[192]{0:T(256)S(1)}, f32[192,2,128]{2,1,0:T(2,128)}, bf16[192,2,128]{2,1,0:T(2,128)(2,1)}) conditional(s32[]{:T(128)} %convert_element_type.170, (f32[192,1728]{1,0:T(8,128)S(1)}, f32[192]{0:T(256)S(1)}) %tuple.180, (s32[]{:T(128)}, s32[]{:T(128)}, pred[]{:T(512)}, pred[]{:T(512)}, ...), branch_computations={%region_5.5_spmd, %region_6.7_spmd.clone} | conditional | flops 343216128 | bytes 17083920 | solution.py:183
  1473.5 7.4 collective-permute-done.3
  1484.1 6.9 collective-permute-start.5
  1494.0 33.2 %conditional.5 = (f32[192,1728]{1,0:T(8,128)S(1)}, f32[192]{0:T(256)S(1)}, f32[192,2,128]{2,1,0:T(2,128)}, bf16[192,2,128]{2,1,0:T(2,128)(2,1)}) conditional(s32[]{:T(128)} %convert_element_type.170, (f32[192,1728]{1,0:T(8,128)S(1)}, f32[192]{0:T(256)S(1)}) %tuple.180, (s32[]{:T(128)}, s32[]{:T(128)}, pred[]{:T(512)}, pred[]{:T(512)}, ...), branch_computations={%region_5.5_spmd, %region_6.7_spmd.clone} | conditional | flops 343216128 | bytes 17083920 | solution.py:183
  1538.1 7.0 collective-permute-start.5
  1548.1 33.2 %conditional.5 = (f32[192,1728]{1,0:T(8,128)S(1)}, f32[192]{0:T(256)S(1)}, f32[192,2,128]{2,1,0:T(2,128)}, bf16[192,2,128]{2,1,0:T(2,128)(2,1)}) conditional(s32[]{:T(128)} %convert_element_type.170, (f32[192,1728]{1,0:T(8,128)S(1)}, f32[192]{0:T(256)S(1)}) %tuple.180, (s32[]{:T(128)}, s32[]{:T(128)}, pred[]{:T(512)}, pred[]{:T(512)}, ...), branch_computations={%region_5.5_spmd, %region_6.7_spmd.clone} | conditional | flops 343216128 | bytes 17083920 | solution.py:183
  1592.1 7.0 collective-permute-start.5
  1602.1 33.2 %conditional.5 = (f32[192,1728]{1,0:T(8,128)S(1)}, f32[192]{0:T(256)S(1)}, f32[192,2,128]{2,1,0:T(2,128)}, bf16[192,2,128]{2,1,0:T(2,128)(2,1)}) conditional(s32[]{:T(128)} %convert_element_type.170, (f32[192,1728]{1,0:T(8,128)S(1)}, f32[192]{0:T(256)S(1)}) %tuple.180, (s32[]{:T(128)}, s32[]{:T(128)}, pred[]{:T(512)}, pred[]{:T(512)}, ...), branch_computations={%region_5.5_spmd, %region_6.7_spmd.clone} | conditional | flops 343216128 | bytes 17083920 | solution.py:183
  1638.1 182.0 %psum.15 = bf16[192]{0:T(256)(128)(2,1)S(1)} all-reduce(bf16[192]{0:T(256)(128)(2,1)S(1)} %convert_element_type.117), channel_id=1, replica_groups=mesh['segment'=8,'lat'=16,'dp'=2] {'lat','dp'}, use_global_device_ids=true, to_apply=%region_10.11 | all-reduce | flops 192 | bytes 768 | tf_op jit(solution)/shard_map/psum | solution.py:199
  1820.6 195.1 %all-reduce.2.cloned.1.call-done = bf16[192,1728]{1,0:T(8,128)(2,1)} async-done(((bf16[192,1728]{1,0:T(8,128)(2,1)}), bf16[192,1728]{1,0:T(8,128)(2,1)}) %all-reduce.2.cloned.1.call-update) | async-done | bytes 663568 | tf_op jit(solution)/shard_map/psum | solution.py:198
  (1342 shorter events, 942.8 us)
Async XLA Ops:
  7.2 2008.6 %all-reduce.2.cloned.1.call-start = ((), (), s32[]{:S(2)}) async-start(), calls=%async_computation | async-start | bytes 1376256 | tf_op jit(solution)/shard_map/psum | solution.py:198
  180.3 9.7 collective-permute-start.1
  334.6 10.1 collective-permute-start.1
  354.7 10.6 collective-permute-start.1
  356.0 9.8 collective-permute-start.2
  392.9 9.6 collective-permute-start.1
  412.2 11.5 collective-permute-start.1
  413.5 10.6 collective-permute-start.2
  434.9 10.9 collective-permute-start.1
  436.2 10.0 collective-permute-start.2
  448.9 9.9 collective-permute-start
  459.0 9.7 collective-permute-start.1
  474.1 10.6 collective-permute-start.3
  486.6 12.7 collective-permute-start.4
  487.9 11.6 collective-permute-start.5
  503.0 37.6 %collective-permute-start.3 = (bf16[192,2,128]{2,1,0:T(2,128)(2,1)}, bf16[192,2,128]{2,1,0:T(2,128)(2,1)S(1)}, u32[]{:S(2)}, u32[]{:S(2)}) collective-permute-start(bf16[192,2,128]{2,1,0:T(2,128)(2,1)} %get-tuple-element.1480), channel_id=1, source_target_pairs={{0,224},{32,0},{64,32},{96,64},{128,96},{160,128},{192,160},{224,1... | collective-permute-start | bytes 294920 | tf_op jit(solution)/shard_map/while/body/eval_jaxpr/ppermute | solution.py:14
  542.6 10.0 collective-permute-start.4
  556.0 37.6 %collective-permute-start.3 = (bf16[192,2,128]{2,1,0:T(2,128)(2,1)}, bf16[192,2,128]{2,1,0:T(2,128)(2,1)S(1)}, u32[]{:S(2)}, u32[]{:S(2)}) collective-permute-start(bf16[192,2,128]{2,1,0:T(2,128)(2,1)} %get-tuple-element.1480), channel_id=1, source_target_pairs={{0,224},{32,0},{64,32},{96,64},{128,96},{160,128},{192,160},{224,1... | collective-permute-start | bytes 294920 | tf_op jit(solution)/shard_map/while/body/eval_jaxpr/ppermute | solution.py:14
  595.6 10.4 collective-permute-start.4
  596.9 10.1 collective-permute-start.5
  610.4 36.1 %collective-permute-start.3 = (bf16[192,2,128]{2,1,0:T(2,128)(2,1)}, bf16[192,2,128]{2,1,0:T(2,128)(2,1)S(1)}, u32[]{:S(2)}, u32[]{:S(2)}) collective-permute-start(bf16[192,2,128]{2,1,0:T(2,128)(2,1)} %get-tuple-element.1480), channel_id=1, source_target_pairs={{0,224},{32,0},{64,32},{96,64},{128,96},{160,128},{192,160},{224,1... | collective-permute-start | bytes 294920 | tf_op jit(solution)/shard_map/while/body/eval_jaxpr/ppermute | solution.py:14
  648.5 11.7 collective-permute-start.4
  649.8 10.4 collective-permute-start.5
  663.7 37.1 %collective-permute-start.3 = (bf16[192,2,128]{2,1,0:T(2,128)(2,1)}, bf16[192,2,128]{2,1,0:T(2,128)(2,1)S(1)}, u32[]{:S(2)}, u32[]{:S(2)}) collective-permute-start(bf16[192,2,128]{2,1,0:T(2,128)(2,1)} %get-tuple-element.1480), channel_id=1, source_target_pairs={{0,224},{32,0},{64,32},{96,64},{128,96},{160,128},{192,160},{224,1... | collective-permute-start | bytes 294920 | tf_op jit(solution)/shard_map/while/body/eval_jaxpr/ppermute | solution.py:14
  702.8 13.6 collective-permute-start.4
  704.1 12.5 collective-permute-start.5
  728.1 10.3 collective-permute-start.4
  729.4 9.6 collective-permute-start.5
  742.5 31.4 %collective-permute-start.3 = (bf16[192,2,128]{2,1,0:T(2,128)(2,1)}, bf16[192,2,128]{2,1,0:T(2,128)(2,1)S(1)}, u32[]{:S(2)}, u32[]{:S(2)}) collective-permute-start(bf16[192,2,128]{2,1,0:T(2,128)(2,1)} %get-tuple-element.1480), channel_id=1, source_target_pairs={{0,224},{32,0},{64,32},{96,64},{128,96},{160,128},{192,160},{224,1... | collective-permute-start | bytes 294920 | tf_op jit(solution)/shard_map/while/body/eval_jaxpr/ppermute | solution.py:14
  775.9 9.9 collective-permute-start.4
  789.2 56.2 %collective-permute-start.3 = (bf16[192,2,128]{2,1,0:T(2,128)(2,1)}, bf16[192,2,128]{2,1,0:T(2,128)(2,1)S(1)}, u32[]{:S(2)}, u32[]{:S(2)}) collective-permute-start(bf16[192,2,128]{2,1,0:T(2,128)(2,1)} %get-tuple-element.1480), channel_id=1, source_target_pairs={{0,224},{32,0},{64,32},{96,64},{128,96},{160,128},{192,160},{224,1... | collective-permute-start | bytes 294920 | tf_op jit(solution)/shard_map/while/body/eval_jaxpr/ppermute | solution.py:14
  847.3 12.7 collective-permute-start.4
  848.6 11.4 collective-permute-start.5
  895.3 11.6 collective-permute-start.3
  908.8 9.4 collective-permute-start.4
  962.6 9.6 collective-permute-start.4
  1015.8 9.4 collective-permute-start.4
  1066.1 13.4 collective-permute-start.4
  1067.4 13.1 collective-permute-start.5
  1084.0 35.4 %collective-permute-start.3 = (bf16[192,2,128]{2,1,0:T(2,128)(2,1)}, bf16[192,2,128]{2,1,0:T(2,128)(2,1)S(1)}, u32[]{:S(2)}, u32[]{:S(2)}) collective-permute-start(bf16[192,2,128]{2,1,0:T(2,128)(2,1)} %get-tuple-element.1480), channel_id=1, source_target_pairs={{0,224},{32,0},{64,32},{96,64},{128,96},{160,128},{192,160},{224,1... | collective-permute-start | bytes 294920 | tf_op jit(solution)/shard_map/while/body/eval_jaxpr/ppermute | solution.py:14
  1121.3 10.6 collective-permute-start.4
  1122.6 10.4 collective-permute-start.5
  1136.4 36.3 %collective-permute-start.3 = (bf16[192,2,128]{2,1,0:T(2,128)(2,1)}, bf16[192,2,128]{2,1,0:T(2,128)(2,1)S(1)}, u32[]{:S(2)}, u32[]{:S(2)}) collective-permute-start(bf16[192,2,128]{2,1,0:T(2,128)(2,1)} %get-tuple-element.1480), channel_id=1, source_target_pairs={{0,224},{32,0},{64,32},{96,64},{128,96},{160,128},{192,160},{224,1... | collective-permute-start | bytes 294920 | tf_op jit(solution)/shard_map/while/body/eval_jaxpr/ppermute | solution.py:14
  1174.7 10.0 collective-permute-start.4
  1176.0 9.7 collective-permute-start.5
  1189.2 37.1 %collective-permute-start.3 = (bf16[192,2,128]{2,1,0:T(2,128)(2,1)}, bf16[192,2,128]{2,1,0:T(2,128)(2,1)S(1)}, u32[]{:S(2)}, u32[]{:S(2)}) collective-permute-start(bf16[192,2,128]{2,1,0:T(2,128)(2,1)} %get-tuple-element.1480), channel_id=1, source_target_pairs={{0,224},{32,0},{64,32},{96,64},{128,96},{160,128},{192,160},{224,1... | collective-permute-start | bytes 294920 | tf_op jit(solution)/shard_map/while/body/eval_jaxpr/ppermute | solution.py:14
  1228.2 10.7 collective-permute-start.4
  1229.5 9.4 collective-permute-start.5
  1242.4 37.4 %collective-permute-start.3 = (bf16[192,2,128]{2,1,0:T(2,128)(2,1)}, bf16[192,2,128]{2,1,0:T(2,128)(2,1)S(1)}, u32[]{:S(2)}, u32[]{:S(2)}) collective-permute-start(bf16[192,2,128]{2,1,0:T(2,128)(2,1)} %get-tuple-element.1480), channel_id=1, source_target_pairs={{0,224},{32,0},{64,32},{96,64},{128,96},{160,128},{192,160},{224,1... | collective-permute-start | bytes 294920 | tf_op jit(solution)/shard_map/while/body/eval_jaxpr/ppermute | solution.py:14
  1281.7 10.0 collective-permute-start.4
  1283.0 9.7 collective-permute-start.5
  1302.3 12.1 collective-permute-start.4
  1303.6 12.7 collective-permute-start.5
  1319.8 29.5 %collective-permute-start.3 = (bf16[192,2,128]{2,1,0:T(2,128)(2,1)}, bf16[192,2,128]{2,1,0:T(2,128)(2,1)S(1)}, u32[]{:S(2)}, u32[]{:S(2)}) collective-permute-start(bf16[192,2,128]{2,1,0:T(2,128)(2,1)} %get-tuple-element.1480), channel_id=1, source_target_pairs={{0,224},{32,0},{64,32},{96,64},{128,96},{160,128},{192,160},{224,1... | collective-permute-start | bytes 294920 | tf_op jit(solution)/shard_map/while/body/eval_jaxpr/ppermute | solution.py:14
  1351.2 10.0 collective-permute-start.4
  1364.7 58.4 %collective-permute-start.3 = (bf16[192,2,128]{2,1,0:T(2,128)(2,1)}, bf16[192,2,128]{2,1,0:T(2,128)(2,1)S(1)}, u32[]{:S(2)}, u32[]{:S(2)}) collective-permute-start(bf16[192,2,128]{2,1,0:T(2,128)(2,1)} %get-tuple-element.1480), channel_id=1, source_target_pairs={{0,224},{32,0},{64,32},{96,64},{128,96},{160,128},{192,160},{224,1... | collective-permute-start | bytes 294920 | tf_op jit(solution)/shard_map/while/body/eval_jaxpr/ppermute | solution.py:14
  1425.1 12.1 collective-permute-start.4
  1426.4 10.8 collective-permute-start.5
  1482.8 9.9 collective-permute-start.4
  1484.1 9.5 collective-permute-start.5
  1536.8 9.9 collective-permute-start.4
  1538.1 9.6 collective-permute-start.5
  1590.8 9.9 collective-permute-start.4
  1592.1 9.6 collective-permute-start.5
  (95 other events, 758.1 us)
Sparse Core Ops, SparseCore 0:
  1638.2 377.5 all-reduce.1
where the time goes:
time: 2040 us; the launch traced here: 2030 us
  starting transfers between devices  759 us (37%)
  waiting for transfers between devices  455 us (22%)
  local copies, waits for them, and re-layouts  373 us (18%)
  other arithmetic  222 us (11%)
  blocking collectives  182 us (9%)
    ppermute x44, starting transfers between devices, passed_along(): return lax.ppermute(value, axis, pairs)  371 us
    ppermute x44, starting transfers between devices, padded_2(): lax.ppermute(lax.slice_in_dim(block, block.shape[dim] - width, None, axis...  331 us
    ppermute x44, waiting for transfers between devices, passed_along(): return lax.ppermute(value, axis, pairs)  237 us
    psum x1, waiting for transfers between devices, per_device(): lax.psum(kernel_sum.astype(jnp.bfloat16), ('lat', 'dp')).astype(jnp.float32)  195 us
    psum x1, blocking collectives, per_device(): lax.psum(bias_sum.astype(jnp.bfloat16), ('lat', 'dp')).astype(jnp.float32)  182 us
    dynamic_slice x132, local copies, waits for them, and re-layouts, put_slot(): previous = lax.dynamic_index_in_dim(buffer, slot, 0, keepdims=False)  105 us
    another operation x80, local copies, waits for them, and re-layouts, back_columns(): stacked = jnp.stack(pieces, axis=0)  68.2 us
    concatenate x48, other arithmetic, back_columns(): pieces.append(jnp.roll(strip, col_tap - 1, axis=2))  63.6 us
  transfers between devices with their start and end apart: 133, of which 81 were waited for; matrix products, arithmetic and copies ran while one was open for 6% of the time, Pallas kernels for 0%

commit v1 on v0

v1 whole, which is shorter than its diff:
```python
import functools
import math

import jax
import jax.numpy as jnp
from jax import lax
from jax.experimental import pallas as pl
from jax.experimental.pallas import tpu as pltpu
from jax.sharding import PartitionSpec as P

STEPS = 2
SECTIONS = 8
APPS = STEPS * SECTIONS
BF = jnp.bfloat16
F32 = jnp.float32
MESH = pl.DeviceIdType.MESH
HALO_UP, HALO_DN = 0, 1


def silu_value(values):
    return values / (1.0 + jnp.exp(-values))


def silu_slope(values):
    sigmoid_v = 1.0 / (1.0 + jnp.exp(-values))
    return sigmoid_v * (1.0 + values * (1.0 - sigmoid_v))


def units_for(lat_count, rows):
    for count in range(min(lat_count, rows // 16), 0, -1):
        if rows % (16 * count) == 0:
            return count
    return 1


def network_kernel(
    dims, x_ref, w_ref, so_ref, sa_ref, gw_ref,
    xc, wall, b2, pbuf, gbuf, sbuf, dwf, cr, cs, r2, r3st, r3, xsem, wss, wrs,
    hss, hrs, oss, ors, crs, crr, r2s, r2r, r3s, r3r, r4s, r4r, r5,
):
    C, W, nz = dims
    K3 = 3 * C
    half = K3 // 2
    part = half // 2
    lanes = w_ref.shape[1]
    nlat = 2 * nz
    nrow = 4 * nz
    nu = units_for(nlat, half)
    ur = half // nu

    seg = lax.axis_index("segment")
    lat = lax.axis_index("lat")
    core = lax.axis_index("dp")
    x_lo, y = seg // 4, lax.rem(seg, 4)
    z, x_hi = lat // 2, lax.rem(lat, 2)
    x = 2 * x_hi + x_lo
    odd = lax.rem(z, 2)
    xr = x + odd * (3 - 2 * x)
    row = 4 * z + xr
    has_up = row > 0
    has_dn = row < nrow - 1

    def at(px, py, pz, pc=core):
        return {"segment": lax.rem(px, 2) * 4 + py, "lat": pz * 2 + px // 2, "dp": pc}

    def holder(r):
        rz = r // 4
        rx = lax.rem(r, 4)
        return at(rx + lax.rem(rz, 2) * (3 - 2 * rx), y, rz)

    up_dev = holder(jnp.maximum(row - 1, 0))
    dn_dev = holder(jnp.minimum(row + 1, nrow - 1))
    other = 1 - core
    partner = {"segment": seg, "lat": lat, "dp": other}
    y_up, y_dn = lax.rem(y + 1, 4), lax.rem(y + 3, 4)
    x_up, x_dn = lax.rem(x + 1, 4), lax.rem(x + 3, 4)

    barrier = pltpu.get_barrier_semaphore()
    for d in range(1, 16):
        dx, dy = d // 4, d % 4
        pl.semaphore_signal(
            barrier, inc=1, device_id=at(lax.rem(x + dx, 4), lax.rem(y + dy, 4), z), device_id_type=MESH
        )
    for d in range(1, nz):
        for hi in range(2):
            peer = {"segment": seg, "lat": lax.rem(z + d, nz) * 2 + hi, "dp": core}
            pl.semaphore_signal(barrier, inc=1, device_id=peer, device_id_type=MESH)
    pl.semaphore_signal(barrier, inc=1, device_id=partner, device_id_type=MESH)
    pl.semaphore_wait(barrier, 15 + 2 * (nz - 1) + 1)

    def remote(src, dst, ssem, rsem, dev):
        return pltpu.make_async_remote_copy(
            src_ref=src, dst_ref=dst, send_sem=ssem, recv_sem=rsem, device_id=dev, device_id_type=MESH
        )

    swap = remote(x_ref, xc, xsem.at[0], xsem.at[1], at(3 - x, y, z))

    @pl.when(odd == 1)
    def _():
        swap.start()

    wall[seg] = w_ref[...].reshape(2, 2, part, lanes)
    sec_dn, sec_up = x_lo * 4 + y_dn, x_lo * 4 + y_up
    sec_far = x_lo * 4 + lax.rem(y + 2, 4)
    sends = []

    def go(copy):
        copy.start()
        sends.append(copy)

    def send_w(index, src, slot, dev):
        go(remote(src, src, wss.at[index], wrs.at[slot], dev))

    dev_yu, dev_yd = at(x, y_up, z), at(x, y_dn, z)
    dev_xu, dev_xd = at(x_up, y, z), at(x_dn, y, z)
    send_w(0, wall.at[seg, core], 0, dev_yu)
    send_w(1, wall.at[seg, core], 1, dev_yd)
    send_w(2, wall.at[seg, core, 0], 4 + 2 * y, dev_xu)
    send_w(3, wall.at[seg, core, 1], 5 + 2 * y, dev_xd)

    def landed(ref, slot):
        pltpu.make_async_copy(ref, ref, wrs.at[slot]).wait()

    def spread(index, sec, sy):
        send_w(index, wall.at[sec, core, 0], 4 + 2 * sy, dev_xu)
        send_w(index + 1, wall.at[sec, core, 1], 5 + 2 * sy, dev_xd)
        send_w(index + 2, wall.at[sec, core], 12 + sec, partner)

    landed(wall.at[sec_dn, core], 0)
    send_w(4, wall.at[sec_dn, core, 0], 2, dev_yu)
    spread(5, sec_dn, y_dn)
    landed(wall.at[sec_up, core], 1)
    send_w(8, wall.at[sec_up, core, 1], 3, dev_yd)
    spread(9, sec_up, y_up)
    landed(wall.at[sec_far, core, 0], 2)
    landed(wall.at[sec_far, core, 1], 3)
    spread(12, sec_far, lax.rem(y + 2, 4))
    for j in range(4):
        sy = lax.rem(y + j, 4)
        sec = (1 - x_lo) * 4 + sy
        landed(wall.at[sec, core, 0], 4 + 2 * sy)
        landed(wall.at[sec, core, 1], 5 + 2 * sy)
        send_w(15 + j, wall.at[sec, core], 12 + sec, partner)
    for j in range(1, 8):
        sec = lax.rem(seg + j, 8)
        landed(wall.at[sec, other], 12 + sec)

    ones = (lax.broadcasted_iota(jnp.int32, (lanes - K3, W), 0) < 2).astype(F32).astype(BF)

    @pl.loop(0, APPS)
    def _(a):
        pbuf[a, K3:, :] = ones

    @pl.when(jnp.logical_not(has_up))
    def _():
        @pl.loop(0, APPS)
        def _(a):
            pbuf[a, 0:C, :] = jnp.zeros((C, W), BF)
            gbuf[a + 1, 0:C, :] = jnp.zeros((C, W), BF)

    @pl.when(jnp.logical_not(has_dn))
    def _():
        @pl.loop(0, APPS)
        def _(a):
            pbuf[a, C : 2 * C, :] = jnp.zeros((C, W), BF)
            gbuf[a + 1, C : 2 * C, :] = jnp.zeros((C, W), BF)

    @pl.when(odd == 1)
    def _():
        swap.wait()

    @pl.when(odd == 0)
    def _():
        xc[...] = x_ref[...]

    sbuf[0] = xc[0]
    gbuf[APPS, 2 * C :, :] = xc[1]

    def halo_copies(buf, slot, step):
        own = buf.at[slot, pl.ds(2 * C, C), :]
        to_up = remote(own, buf.at[slot, pl.ds(C, C), :], hss.at[step, 0], hrs.at[step, 1], up_dev)
        to_dn = remote(own, buf.at[slot, pl.ds(0, C), :], hss.at[step, 1], hrs.at[step, 0], dn_dev)
        return to_up, to_dn

    def halo_start(buf, slot, step):
        to_up, to_dn = halo_copies(buf, slot, step)

        @pl.when(has_up)
        def _():
            to_up.start()

        @pl.when(has_dn)
        def _():
            to_dn.start()

    def halo_wait(buf, slot, step):
        to_up, to_dn = halo_copies(buf, slot, step)

        @pl.when(has_up)
        def _():
            to_up.wait_send()
            pltpu.make_async_copy(buf.at[slot, pl.ds(0, C), :], buf.at[slot, pl.ds(0, C), :], hrs.at[step, 0]).wait()

        @pl.when(has_dn)
        def _():
            to_dn.wait_send()
            pltpu.make_async_copy(buf.at[slot, pl.ds(C, C), :], buf.at[slot, pl.ds(C, C), :], hrs.at[step, 1]).wait()

    out_slot = y * 2 + lax.rem(xr, 2)
    out_lat = 2 * z + xr // 2

    def out_copy(src, dst, which, k):
        dev = {"segment": k, "lat": out_lat, "dp": core}
        return remote(src, dst.at[out_slot], oss.at[which, k], ors.at[which, out_slot], dev)

    def is_self(k):
        return jnp.logical_and(seg == k, out_lat == lat)

    def out_send(src, dst, which, k):
        mine = is_self(k)

        @pl.when(mine)
        def _():
            dst[out_slot] = src[...]

        @pl.when(jnp.logical_not(mine))
        def _():
            out_copy(src, dst, which, k).start()

    def shifted_sum(parts, sign):
        minus, same, plus = parts[0:C], parts[C : 2 * C], parts[2 * C :]
        return same + pltpu.roll(minus, 1 if sign < 0 else W - 1, 1) + pltpu.roll(plus, W - 1 if sign < 0 else 1, 1)

    def forward(a, carry):
        k = lax.rem(a, SECTIONS)
        state = sbuf[a].astype(F32)
        pbuf[a, 2 * C : K3, :] = silu_value(state).astype(BF)
        halo_start(pbuf, a, a)
        own = jnp.dot(
            wall[k, :, :, :, 2 * C :].reshape(K3, lanes - 2 * C), pbuf[a, 2 * C :, :], preferred_element_type=F32
        )
        halo_wait(pbuf, a, a)
        rest = jnp.dot(
            wall[k, :, :, :, 0 : 2 * C].reshape(K3, 2 * C), pbuf[a, 0 : 2 * C, :], preferred_element_type=F32
        )
        sbuf[a + 1] = (state + shifted_sum(own + rest, -1)).astype(BF)

        @pl.when(a >= APPS - SECTIONS)
        def _():
            out_send(sbuf.at[a + 1], so_ref, 0, k)

        return carry

    lax.fori_loop(0, APPS, forward, 0)

    def turned_weights(k):
        for q in range(3):
            flat = wall[k].reshape(K3, lanes)[q * C : (q + 1) * C]
            turned = flat[:, : K3].T
            b2[1, q * C : (q + 1) * C, :] = turned[0:C]
            b2[0, q * C : (q + 1) * C, :] = turned[C : 2 * C]
            b2[2, q * C : (q + 1) * C, :] = turned[2 * C :]

    def tapped(grad):
        wide = grad.astype(F32)
        return jnp.concatenate(
            [pltpu.roll(wide, W - 1, 1).astype(BF), grad, pltpu.roll(wide, 1, 1).astype(BF)], axis=0
        )

    def reduce_pair(k):
        mine = dwf.at[k, core]
        pltpu.make_async_copy(cr.at[k], cr.at[k], crr.at[k]).wait()
        cs[k] = (mine[...].astype(F32) + cr[k].astype(F32)).astype(BF)

        @pl.when(seg == k)
        def _():
            r2[seg] = cs[k]

        @pl.when(seg != k)
        def _():
            remote(cs.at[k], r2.at[seg], r2s.at[k], r2r.at[seg], {"segment": k, "lat": lat, "dp": core}).start()

    def backward(a, with_weights):
        k = lax.rem(a, SECTIONS)
        step = APPS + APPS - 1 - a
        slot = a + 1
        halo_start(gbuf, slot, step)
        grad = gbuf[slot, 2 * C :, :]
        turned_weights(k)
        own = jnp.dot(b2[2], grad, preferred_element_type=F32)
        if with_weights:
            later = a + SECTIONS
            taps = jnp.concatenate([tapped(grad), tapped(gbuf[later + 1, 2 * C :, :])], axis=1)
            acts = jnp.concatenate([pbuf[a], pbuf[later]], axis=1)
            dw = lax.dot_general(taps, acts, (((1,), (1,)), ((), ())), preferred_element_type=F32)
            dwf[k] = dw.astype(BF).reshape(2, half, lanes)
            remote(dwf.at[k, other], cr.at[k], crs.at[k], crr.at[k], partner).start()

            @pl.when(a < SECTIONS - 1)
            def _():
                reduce_pair(k + 1)

        halo_wait(gbuf, slot, step)
        rest = jnp.dot(b2[0], gbuf[slot, 0:C, :], preferred_element_type=F32) + jnp.dot(
            b2[1], gbuf[slot, C : 2 * C, :], preferred_element_type=F32
        )
        slope = silu_slope(sbuf[a].astype(F32))
        adjoint = grad.astype(F32) + slope * shifted_sum(own + rest, 1)
        if not with_weights:
            adjoint = adjoint + jnp.where(a == SECTIONS, xc[2].astype(F32), 0.0)
        gbuf[a, 2 * C :, :] = adjoint.astype(BF)
        if with_weights:
            out_send(gbuf.at[a, pl.ds(2 * C, C), :], sa_ref, 1, k)

    def backward_late(i, carry):
        backward(APPS - 1 - i, False)
        return carry

    def backward_early(i, carry):
        backward(SECTIONS - 1 - i, True)
        return carry

    lax.fori_loop(0, SECTIONS, backward_late, 0)
    lax.fori_loop(0, SECTIONS, backward_early, 0)

    reduce_pair(0)
    total = cs[seg].astype(F32)
    for d in range(1, 8):
        src = lax.rem(seg + d, 8)
        pltpu.make_async_copy(r2.at[src], r2.at[src], r2r.at[src]).wait()
        total = total + r2[src].astype(F32)
    r3st[...] = total.astype(BF).reshape(nu, ur, lanes)
    for u in range(nu):
        @pl.when(lat != u)
        def _():
            remote(
                r3st.at[u], r3.at[lat], r3s.at[u], r3r.at[lat], {"segment": seg, "lat": u, "dp": core}
            ).start()

    @pl.when(lat < nu)
    def _():
        unit = r3st[lat].astype(F32)
        for d in range(1, nlat):
            src = lax.rem(lat + d, nlat)
            pltpu.make_async_copy(r3.at[src], r3.at[src], r3r.at[src]).wait()
            unit = unit + r3[src].astype(F32)
        gw_ref[core, lat] = unit.astype(BF)
        for d in range(1, nlat):
            peer = {"segment": seg, "lat": lax.rem(lat + d, nlat), "dp": core}
            remote(gw_ref.at[core, lat], gw_ref.at[core, lat], r4s.at[d], r4r.at[lat], peer).start()

    for u in range(nu):
        @pl.when(lat != u)
        def _():
            pltpu.make_async_copy(gw_ref.at[core, u], gw_ref.at[core, u], r4r.at[u]).wait()
    last = remote(gw_ref.at[core], gw_ref.at[core], r5.at[0], r5.at[1], partner)
    last.start()

    for copy in sends:
        copy.wait_send()
    for k in range(SECTIONS):
        for which, (dst, src) in enumerate(
            ((so_ref, sbuf.at[APPS - SECTIONS + k + 1]), (sa_ref, gbuf.at[k, pl.ds(2 * C, C), :]))
        ):
            @pl.when(jnp.logical_not(is_self(k)))
            def _():
                out_copy(src, dst, which, k).wait_send()

    for s in range(8):
        sxr = 2 * x_hi + s % 2
        sx = sxr + odd * (3 - 2 * sxr)
        from_self = jnp.logical_and(sx == x, y == s // 2)
        for which, dst in enumerate((so_ref, sa_ref)):
            @pl.when(jnp.logical_not(from_self))
            def _():
                pltpu.make_async_copy(dst.at[s], dst.at[s], ors.at[which, s]).wait()

    for k in range(SECTIONS):
        pltpu.make_async_copy(dwf.at[k, other], dwf.at[k, other], crs.at[k]).wait()

        @pl.when(seg != k)
        def _():
            pltpu.make_async_copy(cs.at[k], cs.at[k], r2s.at[k]).wait()

    for u in range(nu):
        @pl.when(lat != u)
        def _():
            pltpu.make_async_copy(r3st.at[u], r3st.at[u], r3s.at[u]).wait()

    @pl.when(lat < nu)
    def _():
        for d in range(1, nlat):
            pltpu.make_async_copy(gw_ref.at[core, lat], gw_ref.at[core, lat], r4s.at[d]).wait()

    last.wait_send()
    pltpu.make_async_copy(gw_ref.at[other], gw_ref.at[other], r5.at[1]).wait()


def per_device(nz, initial, kernel, bias, cotangent):
    seg = lax.axis_index("segment")
    x_lo, y = seg // 4, lax.rem(seg, 4)
    C, W = initial.shape[1], initial.shape[3]
    K3 = 3 * C
    lanes = -(-(K3 + 2) // 128) * 128
    half, part = K3 // 2, K3 // 4
    nlat = 2 * nz
    nu = units_for(nlat, half)
    ur = half // nu

    stacked = jnp.concatenate([initial[None], cotangent[1:2], cotangent[0:1]], axis=0)
    rows = lax.dynamic_slice(
        stacked, (0, y, 0, x_lo, 0), (3, 1, C, 1, W)
    ).reshape(3, C, W)

    taps = kernel[0].reshape(C, 3, 3, C)
    taps = jnp.concatenate([taps[:, 0:1], taps[:, 2:3], taps[:, 1:2]], axis=1)
    flat = taps.transpose(2, 0, 1, 3).reshape(K3, K3)
    coarse = lax.reduce_precision(bias[0], 8, 7)
    fine = bias[0] - coarse
    pair = jnp.stack([coarse, fine], axis=1).astype(BF)
    side = jnp.pad(pair, ((C, C), (0, lanes - K3 - 2)))
    weights = jnp.concatenate([flat, side], axis=1)

    vm = pl.BlockSpec(memory_space=pltpu.VMEM)
    dma = pltpu.SemaphoreType.DMA
    so, sa, gw = pl.pallas_call(
        functools.partial(network_kernel, (C, W, nz)),
        out_shape=(
            jax.ShapeDtypeStruct((8, C, W), BF),
            jax.ShapeDtypeStruct((8, C, W), BF),
            jax.ShapeDtypeStruct((2, nu, ur, lanes), BF),
        ),
        in_specs=[vm, vm],
        out_specs=(vm, vm, vm),
        scratch_shapes=[
            pltpu.VMEM((3, C, W), BF),
            pltpu.VMEM((SECTIONS, 2, 2, part, lanes), BF),
            pltpu.VMEM((3, K3, C), BF),
            pltpu.VMEM((APPS, lanes, W), BF),
            pltpu.VMEM((APPS + 1, K3, W), BF),
            pltpu.VMEM((APPS + 1, C, W), BF),
            pltpu.VMEM((SECTIONS, 2, half, lanes), BF),
            pltpu.VMEM((SECTIONS, half, lanes), BF),
            pltpu.VMEM((SECTIONS, half, lanes), BF),
            pltpu.VMEM((SECTIONS, half, lanes), BF),
            pltpu.VMEM((nu, ur, lanes), BF),
            pltpu.VMEM((nlat, ur, lanes), BF),
            dma((2,)),
            dma((19,)),
            dma((20,)),
            dma((2 * APPS, 2)),
            dma((2 * APPS, 2)),
            dma((2, SECTIONS)),
            dma((2, 8)),
            dma((SECTIONS,)),
            dma((SECTIONS,)),
            dma((SECTIONS,)),
            dma((SECTIONS,)),
            dma((nu,)),
            dma((nlat,)),
            dma((nlat,)),
            dma((nu,)),
            dma((2,)),
        ],
        compiler_params=pltpu.CompilerParams(
            collective_id=0, has_side_effects=True, vmem_limit_bytes=60 * 2**20
        ),
    )(rows, weights)

    def banded(slots):
        return slots.reshape(4, 2, C, W).transpose(0, 2, 1, 3)[None]

    normalizer = 1.0 / math.sqrt(initial.shape[0] * 2 * initial.shape[2] * nlat * W)
    grads = gw.reshape(K3, lanes).astype(F32) * normalizer
    core_grads = grads[:, :K3].reshape(3, C, 3, C).transpose(1, 2, 0, 3)
    core_grads = jnp.concatenate([core_grads[:, 0:1], core_grads[:, 2:3], core_grads[:, 1:2]], axis=1)
    return (
        banded(so),
        banded(sa).astype(F32),
        core_grads.reshape(1, C, 9, C),
        grads[C : 2 * C, K3][None],
    )


def solution(mesh):
    nz = mesh.shape["lat"] // 2
    return jax.shard_map(
        functools.partial(per_device, nz),
        mesh=mesh,
        in_specs=(
            P("dp", None, "lat", None),
            P("segment", None, None, None),
            P("segment", None),
            P(None, "dp", None, "lat", None),
        ),
        out_specs=(
            P("segment", "dp", None, "lat", None),
            P("segment", "dp", None, "lat", None),
            P("segment", None, None, None),
            P("segment", None),
        ),
        check_vma=False,
    )
```

time: 2040 us -> 291 us (0.14)
  starting transfers between devices: 759 us -> 0 us
  waiting for transfers between devices: 455 us -> 0 us
  local copies, waits for them, and re-layouts: 373 us -> 17.6 us
  Pallas kernels: 0 us -> 265 us
  other arithmetic: 222 us -> 6.53 us
  blocking collectives: 182 us -> 0 us
    ppermute x132 -> x0, starting transfers between devices: 759 us -> none  [the longest x44 371 us: passed_along(): return lax.ppermute(value, axis, pairs)]
    pallas_call x0 -> x1, Pallas kernels: none -> 265 us  [per_device(): pl.pallas_call(functools.partial(network_kernel, (C, W, nz)), out_shape=(...]
    ppermute x132 -> x0, waiting for transfers between devices: 259 us -> none  [the longest x44 237 us: passed_along(): return lax.ppermute(value, axis, pairs)]
    psum x1 -> x0, waiting for transfers between devices: 195 us -> none  [per_device(): lax.psum(kernel_sum.astype(jnp.bfloat16), ('lat', 'dp')).astype(jnp.float32)]
    psum x1 -> x0, blocking collectives: 182 us -> none  [per_device(): lax.psum(bias_sum.astype(jnp.bfloat16), ('lat', 'dp')).astype(jnp.float32)]
    another operation x149 -> x1, local copies, waits for them, and re-layouts: 111 us -> 0.15 us  [per_device(): pair = jnp.stack([coarse, fine], axis=1).astype(BF)]
    dynamic_slice x132 -> x0, local copies, waits for them, and re-layouts: 105 us -> none  [put_slot(): previous = lax.dynamic_index_in_dim(buffer, slot, 0, keepdims=False)]
    concatenate x92 -> x2, other arithmetic: 71.5 us -> 2.74 us  [the longest x1 1.77 us: per_device(): jnp.concatenate([core_grads[:, 0:1], core_grads[:, 2:3], core_grads[:, 1:...]
  transfers between devices with their start and end apart: 133 -> 0, of which waited for: 81 -> 0; matrix products, arithmetic and copies ran while one was open for 6% -> 0% of each run, Pallas kernels for 0% -> 0%
where the time goes in v1:
time: 291 us; the launch traced here: 290 us
  Pallas kernels  265 us (91%)
  local copies, waits for them, and re-layouts  17.6 us (6%)
  other arithmetic  6.53 us (2%)
    pallas_call x1, Pallas kernels, per_device(): pl.pallas_call(functools.partial(network_kernel, (C, W, nz)), out_shape=(...  265 us

profile of v1, /device:TPU:1, one launch (start us, length us, event | category | flops | bytes accessed | tf_op | source)
XLA Modules:
  0.0 290.3 jit_solution(14934503259346232038)
XLA Ops:
  0.7 0.7 reduce-precision_convert_fusion
  1.4 0.1 copy.43
  1.5 1.1 copy.59
  2.6 1.7 fusion.8
  4.2 0.0 copy-start.1
  4.2 0.1 copy.48
  4.3 0.1 copy.49
  4.4 0.7 fusion.4.x_ref
  5.1 0.4 copy-done.1
  5.5 0.1 fusion.7
  5.5 0.5 copy.50
  6.0 0.5 copy.51
  6.5 0.5 copy.52
  6.9 2.2 maximum_bitcast_fusion
  9.2 0.9 reshape.56
  10.1 1.0 fusion.1.w_ref
  11.1 265.3 %shard_map.75 = (bf16[8,192,128]{2,1,0:T(8,128)(2,1)}, bf16[8,192,128]{2,1,0:T(8,128)(2,1)}, bf16[2,9,32,640]{3,2,1,0:T(8,128)(2,1)}) custom-call(bf16[3,192,128]{2,1,0:T(8,128)(2,1)} %fusion.4.x_ref, bf16[576,640]{1,0:T(8,128)(2,1)} %fusion.1.w_ref), custom_call_target="tpu_custom_call" | custom-call | tf_op jit(solution)/shard_map/pallas_call | solution.py:426
  276.4 0.0 copy-start.2
  276.4 2.2 copy.58
  278.6 2.3 copy.57
  280.9 0.0 copy-done.2
  280.9 0.2 convert_multiply_fusion
  281.1 0.0 copy-start
  281.1 1.1 copy-done
  282.2 0.1 slice.47
  282.3 0.6 copy.53
  282.9 2.8 reshape.58
  285.7 1.2 fusion.6
  287.0 1.8 pad_maximum_fusion
  288.7 1.5 copy.46
  (1 shorter events, 0.0 us)
Async XLA Ops:
  4.2 1.2 copy-start.1
  276.4 4.5 %copy-start.2 = (bf16[2,9,32,640]{3,2,1,0:T(8,128)(2,1)S(1)}, bf16[2,9,32,640]{3,2,1,0:T(8,128)(2,1)}, u32[]{:S(2)}) copy-start(bf16[2,9,32,640]{3,2,1,0:T(8,128)(2,1)} %get-tuple-element.9) | copy-start | bytes 2211844
  281.1 1.1 copy-start

commit v2 on v1

--- a/solution.py
+++ b/solution.py
@@ -26,17 +26,14 @@
     return sigmoid_v * (1.0 + values * (1.0 - sigmoid_v))
 
 
-def units_for(lat_count, rows):
-    for count in range(min(lat_count, rows // 16), 0, -1):
-        if rows % (16 * count) == 0:
-            return count
-    return 1
+PIECES = 6
+UNITS = 3
 
 
 def network_kernel(
     dims, x_ref, w_ref, so_ref, sa_ref, gw_ref,
-    xc, wall, b2, pbuf, gbuf, sbuf, dwf, cr, cs, r2, r3st, r3, xsem, wss, wrs,
-    hss, hrs, oss, ors, crs, crr, r2s, r2r, r3s, r3r, r4s, r4r, r5,
+    xc, wall, b2, pbuf, gbuf, sbuf, dwf, cr, cs, r2, st2, r3, red, xsem, wss, wrs,
+    hss, hrs, oss, ors, crs, crr, r2s, r2r, r3s, r3r, r4s, r4r, r5s, r5r, r6,
 ):
     C, W, nz = dims
     K3 = 3 * C
@@ -45,8 +42,7 @@
     lanes = w_ref.shape[1]
     nlat = 2 * nz
     nrow = 4 * nz
-    nu = units_for(nlat, half)
-    ur = half // nu
+    piece = half // PIECES
 
     seg = lax.axis_index("segment")
     lat = lax.axis_index("lat")
@@ -267,18 +263,89 @@
             [pltpu.roll(wide, W - 1, 1).astype(BF), grad, pltpu.roll(wide, 1, 1).astype(BF)], axis=0
         )
 
-    def reduce_pair(k):
-        mine = dwf.at[k, core]
+    def pair_and_scatter(k):
         pltpu.make_async_copy(cr.at[k], cr.at[k], crr.at[k]).wait()
-        cs[k] = (mine[...].astype(F32) + cr[k].astype(F32)).astype(BF)
-
-        @pl.when(seg == k)
-        def _():
-            r2[seg] = cs[k]
-
-        @pl.when(seg != k)
-        def _():
-            remote(cs.at[k], r2.at[seg], r2s.at[k], r2r.at[seg], {"segment": k, "lat": lat, "dp": core}).start()
+        for jx in range(2):
+            for jy in range(3):
+                j = 3 * jx + jy
+                cs[k, j] = (dwf[k, core, j].astype(F32) + cr[k, j].astype(F32)).astype(BF)
+                near = x_lo == jx
+                far_x = lax.rem(x + (1 if jy % 2 == 0 else 3), 4)
+                home = at(jnp.where(near, x, far_x), jy, z)
+                slot = jnp.where(near, y, 4 + y)
+                mine = jnp.logical_and(near, y == jy)
+
+                @pl.when(mine)
+                def _():
+                    r2[k, slot] = cs[k, j]
+
+                @pl.when(jnp.logical_not(mine))
+                def _():
+                    remote(cs.at[k, j], r2.at[k, slot], r2s.at[k, j], r2r.at[k, slot], home).start()
+
+    def unit_lat(k, u):
+        return lax.rem((nlat // 3) * u + 2 * k, nlat)
+
+    def sum_and_scatter(k):
+        @pl.when(y < 3)
+        def _():
+            total = r2[k, y].astype(F32)
+            for d in range(1, 4):
+                src = lax.rem(y + d, 4)
+                pltpu.make_async_copy(r2.at[k, src], r2.at[k, src], r2r.at[k, src]).wait()
+                total = total + r2[k, src].astype(F32)
+            for src in range(4, 8):
+                pltpu.make_async_copy(r2.at[k, src], r2.at[k, src], r2r.at[k, src]).wait()
+                total = total + r2[k, src].astype(F32)
+            st2[k] = total.astype(BF).reshape(UNITS, piece // UNITS, lanes)
+            for u in range(UNITS):
+                goal = unit_lat(k, u)
+
+                @pl.when(goal != lat)
+                def _():
+                    dev = {"segment": seg, "lat": goal, "dp": core}
+                    remote(st2.at[k, u], r3.at[k, lat], r3s.at[k, u], r3r.at[k, lat], dev).start()
+
+    def lat_sum(k):
+        for u in range(UNITS):
+            @pl.when(jnp.logical_and(y < 3, unit_lat(k, u) == lat))
+            def _():
+                unit = st2[k, u].astype(F32)
+                for d in range(1, nlat):
+                    src = lax.rem(lat + d, nlat)
+                    pltpu.make_async_copy(r3.at[k, src], r3.at[k, src], r3r.at[k, src]).wait()
+                    unit = unit + r3[k, src].astype(F32)
+                red[k, u] = unit.astype(BF)
+                for d in range(1, nlat):
+                    dev = {"segment": seg, "lat": lax.rem(lat + d, nlat), "dp": core}
+                    remote(red.at[k, u], red.at[k, u], r4s.at[k, d], r4r.at[k, u], dev).start()
+
+    my_piece = 3 * x_lo + jnp.minimum(y, 2)
+
+    def deliver(k):
+        @pl.when(y < 3)
+        def _():
+            for u in range(UNITS):
+                @pl.when(unit_lat(k, u) != lat)
+                def _():
+                    pltpu.make_async_copy(red.at[k, u], red.at[k, u], r4r.at[k, u]).wait()
+
+            @pl.when(seg == k)
+            def _():
+                gw_ref[core, my_piece] = red[k]
+
+            @pl.when(seg != k)
+            def _():
+                dev = {"segment": k, "lat": lat, "dp": core}
+                remote(red.at[k], gw_ref.at[core, my_piece], r5s.at[k], r5r.at[my_piece], dev).start()
+
+    def staged(a):
+        for lag, stage in ((1, pair_and_scatter), (3, sum_and_scatter), (5, lat_sum), (7, deliver)):
+            k = a + lag
+
+            @pl.when(jnp.logical_and(k >= 0, k < SECTIONS))
+            def _():
+                stage(k)
 
     def backward(a, with_weights):
         k = lax.rem(a, SECTIONS)
@@ -293,12 +360,9 @@
             taps = jnp.concatenate([tapped(grad), tapped(gbuf[later + 1, 2 * C :, :])], axis=1)
             acts = jnp.concatenate([pbuf[a], pbuf[later]], axis=1)
             dw = lax.dot_general(taps, acts, (((1,), (1,)), ((), ())), preferred_element_type=F32)
-            dwf[k] = dw.astype(BF).reshape(2, half, lanes)
+            dwf[k] = dw.astype(BF).reshape(2, PIECES, piece, lanes)
             remote(dwf.at[k, other], cr.at[k], crs.at[k], crr.at[k], partner).start()
-
-            @pl.when(a < SECTIONS - 1)
-            def _():
-                reduce_pair(k + 1)
+            staged(a)
 
         halo_wait(gbuf, slot, step)
         rest = jnp.dot(b2[0], gbuf[slot, 0:C, :], preferred_element_type=F32) + jnp.dot(
@@ -323,37 +387,16 @@
     lax.fori_loop(0, SECTIONS, backward_late, 0)
     lax.fori_loop(0, SECTIONS, backward_early, 0)
 
-    reduce_pair(0)
-    total = cs[seg].astype(F32)
-    for d in range(1, 8):
-        src = lax.rem(seg + d, 8)
-        pltpu.make_async_copy(r2.at[src], r2.at[src], r2r.at[src]).wait()
-        total = total + r2[src].astype(F32)
-    r3st[...] = total.astype(BF).reshape(nu, ur, lanes)
-    for u in range(nu):
-        @pl.when(lat != u)
-        def _():
-            remote(
-                r3st.at[u], r3.at[lat], r3s.at[u], r3r.at[lat], {"segment": seg, "lat": u, "dp": core}
-            ).start()
-
-    @pl.when(lat < nu)
-    def _():
-        unit = r3st[lat].astype(F32)
-        for d in range(1, nlat):
-            src = lax.rem(lat + d, nlat)
-            pltpu.make_async_copy(r3.at[src], r3.at[src], r3r.at[src]).wait()
-            unit = unit + r3[src].astype(F32)
-        gw_ref[core, lat] = unit.astype(BF)
-        for d in range(1, nlat):
-            peer = {"segment": seg, "lat": lax.rem(lat + d, nlat), "dp": core}
-            remote(gw_ref.at[core, lat], gw_ref.at[core, lat], r4s.at[d], r4r.at[lat], peer).start()
-
-    for u in range(nu):
-        @pl.when(lat != u)
-        def _():
-            pltpu.make_async_copy(gw_ref.at[core, u], gw_ref.at[core, u], r4r.at[u]).wait()
-    last = remote(gw_ref.at[core], gw_ref.at[core], r5.at[0], r5.at[1], partner)
+    def drain(i, carry):
+        staged(-1 - i)
+        return carry
+
+    lax.fori_loop(0, 7, drain, 0)
+    for j in range(PIECES):
+        @pl.when(seg != (j // 3) * 4 + j % 3)
+        def _():
+            pltpu.make_async_copy(gw_ref.at[core, j], gw_ref.at[core, j], r5r.at[j]).wait()
+    last = remote(gw_ref.at[core], gw_ref.at[core], r6.at[0], r6.at[1], partner)
     last.start()
 
     for copy in sends:
@@ -375,25 +418,36 @@
             def _():
                 pltpu.make_async_copy(dst.at[s], dst.at[s], ors.at[which, s]).wait()
 
-    for k in range(SECTIONS):
+    def ended(k, carry):
         pltpu.make_async_copy(dwf.at[k, other], dwf.at[k, other], crs.at[k]).wait()
-
-        @pl.when(seg != k)
-        def _():
-            pltpu.make_async_copy(cs.at[k], cs.at[k], r2s.at[k]).wait()
-
-    for u in range(nu):
-        @pl.when(lat != u)
-        def _():
-            pltpu.make_async_copy(r3st.at[u], r3st.at[u], r3s.at[u]).wait()
-
-    @pl.when(lat < nu)
-    def _():
-        for d in range(1, nlat):
-            pltpu.make_async_copy(gw_ref.at[core, lat], gw_ref.at[core, lat], r4s.at[d]).wait()
-
+        for j in range(PIECES):
+            @pl.when(seg != (j // 3) * 4 + j % 3)
+            def _():
+                pltpu.make_async_copy(cs.at[k, j], cs.at[k, j], r2s.at[k, j]).wait()
+
+        @pl.when(y < 3)
+        def _():
+            for u in range(UNITS):
+                mine = unit_lat(k, u) == lat
+
+                @pl.when(jnp.logical_not(mine))
+                def _():
+                    pltpu.make_async_copy(st2.at[k, u], st2.at[k, u], r3s.at[k, u]).wait()
+
+                @pl.when(mine)
+                def _():
+                    for d in range(1, nlat):
+                        pltpu.make_async_copy(red.at[k, u], red.at[k, u], r4s.at[k, d]).wait()
+
+            @pl.when(seg != k)
+            def _():
+                pltpu.make_async_copy(red.at[k], red.at[k], r5s.at[k]).wait()
+
+        return carry
+
+    lax.fori_loop(0, SECTIONS, ended, 0)
     last.wait_send()
-    pltpu.make_async_copy(gw_ref.at[other], gw_ref.at[other], r5.at[1]).wait()
+    pltpu.make_async_copy(gw_ref.at[other], gw_ref.at[other], r6.at[1]).wait()
 
 
 def per_device(nz, initial, kernel, bias, cotangent):
@@ -404,8 +458,8 @@
     lanes = -(-(K3 + 2) // 128) * 128
     half, part = K3 // 2, K3 // 4
     nlat = 2 * nz
-    nu = units_for(nlat, half)
-    ur = half // nu
+    piece = half // PIECES
+    unit = piece // UNITS
 
     stacked = jnp.concatenate([initial[None], cotangent[1:2], cotangent[0:1]], axis=0)
     rows = lax.dynamic_slice(
@@ -428,7 +482,7 @@
         out_shape=(
             jax.ShapeDtypeStruct((8, C, W), BF),
             jax.ShapeDtypeStruct((8, C, W), BF),
-            jax.ShapeDtypeStruct((2, nu, ur, lanes), BF),
+            jax.ShapeDtypeStruct((2, PIECES, UNITS, unit, lanes), BF),
         ),
         in_specs=[vm, vm],
         out_specs=(vm, vm, vm),
@@ -439,12 +493,13 @@
             pltpu.VMEM((APPS, lanes, W), BF),
             pltpu.VMEM((APPS + 1, K3, W), BF),
             pltpu.VMEM((APPS + 1, C, W), BF),
-            pltpu.VMEM((SECTIONS, 2, half, lanes), BF),
-            pltpu.VMEM((SECTIONS, half, lanes), BF),
-            pltpu.VMEM((SECTIONS, half, lanes), BF),
-            pltpu.VMEM((SECTIONS, half, lanes), BF),
-            pltpu.VMEM((nu, ur, lanes), BF),
-            pltpu.VMEM((nlat, ur, lanes), BF),
+            pltpu.VMEM((SECTIONS, 2, PIECES, piece, lanes), BF),
+            pltpu.VMEM((SECTIONS, PIECES, piece, lanes), BF),
+            pltpu.VMEM((SECTIONS, PIECES, piece, lanes), BF),
+            pltpu.VMEM((SECTIONS, 8, piece, lanes), BF),
+            pltpu.VMEM((SECTIONS, UNITS, unit, lanes), BF),
+            pltpu.VMEM((SECTIONS, nlat, unit, lanes), BF),
+            pltpu.VMEM((SECTIONS, UNITS, unit, lanes), BF),
             dma((2,)),
             dma((19,)),
             dma((20,)),
@@ -454,12 +509,14 @@
             dma((2, 8)),
             dma((SECTIONS,)),
             dma((SECTIONS,)),
+            dma((SECTIONS, PIECES)),
+            dma((SECTIONS, 8)),
+            dma((SECTIONS, UNITS)),
+            dma((SECTIONS, nlat)),
+            dma((SECTIONS, nlat)),
+            dma((SECTIONS, UNITS)),
             dma((SECTIONS,)),
-            dma((SECTIONS,)),
-            dma((nu,)),
-            dma((nlat,)),
-            dma((nlat,)),
-            dma((nu,)),
+            dma((PIECES,)),
             dma((2,)),
         ],
         compiler_params=pltpu.CompilerParams(

time: 291 us -> 252 us (0.87)
  Pallas kernels: 265 us -> 227 us
    pallas_call x1, Pallas kernels: 265 us -> 227 us  [per_device(): pl.pallas_call(functools.partial(network_kernel, (C, W, nz)), out_shape=(...]
where the time goes in v2:
time: 252 us
  Pallas kernels  227 us (90%)
  local copies, waits for them, and re-layouts  17.6 us (7%)
  other arithmetic  6.49 us (3%)
    pallas_call x1, Pallas kernels, per_device(): pl.pallas_call(functools.partial(network_kernel, (C, W, nz)), out_shape=(...  227 us

profile of v2, /device:TPU:1, one launch (start us, length us, event | category | flops | bytes accessed | tf_op | source)
XLA Modules:
  0.0 252.1 jit_solution(1770785309523038972)
XLA Ops:
  0.7 0.7 reduce-precision_convert_fusion
  1.4 0.1 copy.43
  1.5 1.1 copy.59
  2.6 1.7 fusion.8
  4.2 0.0 copy-start.1
  4.2 0.1 copy.48
  4.3 0.1 copy.49
  4.4 0.7 fusion.4.x_ref
  5.1 0.4 copy-done.1
  5.5 0.1 fusion.7
  5.5 0.5 copy.50
  6.0 0.5 copy.51
  6.5 0.5 copy.52
  6.9 2.2 maximum_bitcast_fusion
  9.2 0.9 reshape.56
  10.1 1.0 fusion.1.w_ref
  11.1 227.2 %shard_map.75 = (bf16[8,192,128]{2,1,0:T(8,128)(2,1)}, bf16[8,192,128]{2,1,0:T(8,128)(2,1)}, bf16[2,6,3,16,640]{4,3,2,1,0:T(8,128)(2,1)}) custom-call(bf16[3,192,128]{2,1,0:T(8,128)(2,1)} %fusion.4.x_ref, bf16[576,640]{1,0:T(8,128)(2,1)} %fusion.1.w_ref), custom_call_target="tpu_custom_call" | custom-call | tf_op jit(solution)/shard_map/pallas_call | solution.py:480
  238.2 0.0 copy-start.2
  238.2 2.2 copy.58
  240.5 2.3 copy.57
  242.7 0.0 copy-done.2
  242.7 0.1 convert_multiply_fusion
  242.9 0.0 copy-start
  242.9 1.1 copy-done
  244.0 0.1 slice.47
  244.1 0.6 copy.53
  244.7 2.8 %reshape.58 = f32[3,192,3,192]{3,2,1,0:T(4,128)S(1)} reshape(f32[576,576]{1,0:T(8,128)} %bitcast.31) | data formatting | bytes 2654208 | tf_op jit(solution)/shard_map/reshape | solution.py:532
  247.6 1.2 fusion.6
  248.8 1.8 pad_maximum_fusion
  250.6 1.5 copy.46
  (1 shorter events, 0.0 us)
Async XLA Ops:
  4.2 1.2 copy-start.1
  238.2 4.5 %copy-start.2 = (bf16[2,6,3,16,640]{4,3,2,1,0:T(8,128)(2,1)S(1)}, bf16[2,6,3,16,640]{4,3,2,1,0:T(8,128)(2,1)}, u32[]{:S(2)}) copy-start(bf16[2,6,3,16,640]{4,3,2,1,0:T(8,128)(2,1)} %get-tuple-element.9) | copy-start | bytes 2211844
  242.9 1.1 copy-start

commit v3 on v2

--- a/solution.py
+++ b/solution.py
@@ -51,8 +51,9 @@
     z, x_hi = lat // 2, lax.rem(lat, 2)
     x = 2 * x_hi + x_lo
     odd = lax.rem(z, 2)
-    xr = x + odd * (3 - 2 * x)
-    row = 4 * z + xr
+    held = lax.rem(x_lo + x_hi, 2)
+    band = 2 * z + lax.rem(x_hi + odd, 2)
+    row = 2 * band + core
     has_up = row > 0
     has_dn = row < nrow - 1
 
@@ -60,9 +61,10 @@
         return {"segment": lax.rem(px, 2) * 4 + py, "lat": pz * 2 + px // 2, "dp": pc}
 
     def holder(r):
-        rz = r // 4
-        rx = lax.rem(r, 4)
-        return at(rx + lax.rem(rz, 2) * (3 - 2 * rx), y, rz)
+        r_band = r // 2
+        rz = r_band // 2
+        hi = lax.rem(r_band + rz, 2)
+        return {"segment": lax.rem(held + hi, 2) * 4 + y, "lat": rz * 2 + hi, "dp": lax.rem(r, 2)}
 
     up_dev = holder(jnp.maximum(row - 1, 0))
     dn_dev = holder(jnp.minimum(row + 1, nrow - 1))
@@ -72,28 +74,53 @@
     x_up, x_dn = lax.rem(x + 1, 4), lax.rem(x + 3, 4)
 
     barrier = pltpu.get_barrier_semaphore()
-    for d in range(1, 16):
-        dx, dy = d // 4, d % 4
-        pl.semaphore_signal(
-            barrier, inc=1, device_id=at(lax.rem(x + dx, 4), lax.rem(y + dy, 4), z), device_id_type=MESH
-        )
+    for d in range(1, 32):
+        dx, dy, dc = d // 8, (d // 2) % 4, d % 2
+        peer = at(lax.rem(x + dx, 4), lax.rem(y + dy, 4), z, lax.rem(core + dc, 2))
+        pl.semaphore_signal(barrier, inc=1, device_id=peer, device_id_type=MESH)
     for d in range(1, nz):
         for hi in range(2):
             peer = {"segment": seg, "lat": lax.rem(z + d, nz) * 2 + hi, "dp": core}
             pl.semaphore_signal(barrier, inc=1, device_id=peer, device_id_type=MESH)
-    pl.semaphore_signal(barrier, inc=1, device_id=partner, device_id_type=MESH)
-    pl.semaphore_wait(barrier, 15 + 2 * (nz - 1) + 1)
+    for d in (1, nz - 1):
+        peer = {"segment": seg, "lat": lax.rem(z + d, nz) * 2 + x_hi, "dp": other}
+        pl.semaphore_signal(barrier, inc=1, device_id=peer, device_id_type=MESH)
+    pl.semaphore_wait(barrier, 31 + 2 * (nz - 1) + 2)
 
     def remote(src, dst, ssem, rsem, dev):
         return pltpu.make_async_remote_copy(
             src_ref=src, dst_ref=dst, send_sem=ssem, recv_sem=rsem, device_id=dev, device_id_type=MESH
         )
 
-    swap = remote(x_ref, xc, xsem.at[0], xsem.at[1], at(3 - x, y, z))
-
-    @pl.when(odd == 1)
+    giver = core == held
+    stays = jnp.logical_and(giver, odd == 0)
+    home_x = x + odd * (3 - 2 * x)
+
+    def given(r, what):
+        span = pl.ds(0, 1) if what == 0 else pl.ds(1, 2)
+        return remote(
+            x_ref.at[r, span], xc.at[span], xsem.at[0, 2 * r + what], xsem.at[1, what], at(home_x, y, z, r)
+        )
+
+    def leaves(r):
+        return jnp.logical_and(giver, jnp.logical_or(odd == 1, core != r))
+
+    for what in range(2):
+        for r in range(2):
+            @pl.when(leaves(r))
+            def _():
+                given(r, what).start()
+
+    @pl.when(stays)
     def _():
-        swap.start()
+        xc[...] = x_ref[core]
+
+    def rows_wait(what):
+        span = pl.ds(0, 1) if what == 0 else pl.ds(1, 2)
+
+        @pl.when(jnp.logical_not(stays))
+        def _():
+            pltpu.make_async_copy(xc.at[span], xc.at[span], xsem.at[1, what]).wait()
 
     wall[seg] = w_ref[...].reshape(2, 2, part, lanes)
     sec_dn, sec_up = x_lo * 4 + y_dn, x_lo * 4 + y_up
@@ -161,16 +188,8 @@
             pbuf[a, C : 2 * C, :] = jnp.zeros((C, W), BF)
             gbuf[a + 1, C : 2 * C, :] = jnp.zeros((C, W), BF)
 
-    @pl.when(odd == 1)
-    def _():
-        swap.wait()
-
-    @pl.when(odd == 0)
-    def _():
-        xc[...] = x_ref[...]
-
+    rows_wait(0)
     sbuf[0] = xc[0]
-    gbuf[APPS, 2 * C :, :] = xc[1]
 
     def halo_copies(buf, slot, step):
         own = buf.at[slot, pl.ds(2 * C, C), :]
@@ -202,15 +221,14 @@
             to_dn.wait_send()
             pltpu.make_async_copy(buf.at[slot, pl.ds(C, C), :], buf.at[slot, pl.ds(C, C), :], hrs.at[step, 1]).wait()
 
-    out_slot = y * 2 + lax.rem(xr, 2)
-    out_lat = 2 * z + xr // 2
+    out_slot = y * 2 + core
 
     def out_copy(src, dst, which, k):
-        dev = {"segment": k, "lat": out_lat, "dp": core}
+        dev = {"segment": k, "lat": band, "dp": held}
         return remote(src, dst.at[out_slot], oss.at[which, k], ors.at[which, out_slot], dev)
 
     def is_self(k):
-        return jnp.logical_and(seg == k, out_lat == lat)
+        return jnp.logical_and(seg == k, stays)
 
     def out_send(src, dst, which, k):
         mine = is_self(k)
@@ -248,6 +266,9 @@
         return carry
 
     lax.fori_loop(0, APPS, forward, 0)
+
+    rows_wait(1)
+    gbuf[APPS, 2 * C :, :] = xc[1]
 
     def turned_weights(k):
         for q in range(3):
@@ -409,10 +430,14 @@
             def _():
                 out_copy(src, dst, which, k).wait_send()
 
+    for what in range(2):
+        for r in range(2):
+            @pl.when(leaves(r))
+            def _():
+                given(r, what).wait_send()
+
     for s in range(8):
-        sxr = 2 * x_hi + s % 2
-        sx = sxr + odd * (3 - 2 * sxr)
-        from_self = jnp.logical_and(sx == x, y == s // 2)
+        from_self = jnp.logical_and(stays, jnp.logical_and(core == s % 2, y == s // 2))
         for which, dst in enumerate((so_ref, sa_ref)):
             @pl.when(jnp.logical_not(from_self))
             def _():
@@ -451,8 +476,7 @@
 
 
 def per_device(nz, initial, kernel, bias, cotangent):
-    seg = lax.axis_index("segment")
-    x_lo, y = seg // 4, lax.rem(seg, 4)
+    y = lax.rem(lax.axis_index("segment"), 4)
     C, W = initial.shape[1], initial.shape[3]
     K3 = 3 * C
     lanes = -(-(K3 + 2) // 128) * 128
@@ -463,8 +487,8 @@
 
     stacked = jnp.concatenate([initial[None], cotangent[1:2], cotangent[0:1]], axis=0)
     rows = lax.dynamic_slice(
-        stacked, (0, y, 0, x_lo, 0), (3, 1, C, 1, W)
-    ).reshape(3, C, W)
+        stacked, (0, y, 0, 0, 0), (3, 1, C, 2, W)
+    ).reshape(3, C, 2, W).transpose(2, 0, 1, 3)
 
     taps = kernel[0].reshape(C, 3, 3, C)
     taps = jnp.concatenate([taps[:, 0:1], taps[:, 2:3], taps[:, 1:2]], axis=1)
@@ -500,7 +524,7 @@
             pltpu.VMEM((SECTIONS, UNITS, unit, lanes), BF),
             pltpu.VMEM((SECTIONS, nlat, unit, lanes), BF),
             pltpu.VMEM((SECTIONS, UNITS, unit, lanes), BF),
-            dma((2,)),
+            dma((2, 4)),
             dma((19,)),
             dma((20,)),
             dma((2 * APPS, 2)),

time: 252 us -> 241 us (0.956)
  Pallas kernels: 227 us -> 217 us
    pallas_call x1, Pallas kernels: 227 us -> 217 us  [per_device(): pl.pallas_call(functools.partial(network_kernel, (C, W, nz)), out_shape=(...]
where the time goes in v3:
time: 241 us
  Pallas kernels  217 us (90%)
  local copies, waits for them, and re-layouts  16.9 us (7%)
  other arithmetic  6.35 us (3%)
    pallas_call x1, Pallas kernels, per_device(): pl.pallas_call(functools.partial(network_kernel, (C, W, nz)), out_shape=(...  217 us

profile of v3, /device:TPU:1, one launch (start us, length us, event | category | flops | bytes accessed | tf_op | source)
XLA Modules:
  0.0 241.1 jit_solution(6673044858137936541)
XLA Ops:
  0.6 0.0 copy-start.3
  0.6 0.7 reduce-precision_convert_fusion
  1.4 0.1 copy.38
  1.5 0.0 copy-start.1
  1.6 1.7 fusion.7
  3.3 0.0 copy-done.3
  3.3 0.5 fusion.3
  3.8 0.8 copy.52
  4.6 0.0 copy-done.1
  4.6 0.1 fusion.6
  4.6 0.5 copy.43
  5.1 0.5 copy.44
  5.6 0.5 copy.45
  6.0 2.2 maximum_bitcast_fusion
  8.3 0.9 reshape.56
  9.2 1.0 fusion.1.w_ref
  10.2 217.0 %shard_map.75 = (bf16[8,192,128]{2,1,0:T(8,128)(2,1)}, bf16[8,192,128]{2,1,0:T(8,128)(2,1)}, bf16[2,6,3,16,640]{4,3,2,1,0:T(8,128)(2,1)}) custom-call(bf16[2,3,192,128]{3,2,1,0:T(8,128)(2,1)} %bitcast.34, bf16[576,640]{1,0:T(8,128)(2,1)} %fusion.1.w_ref), custom_call_target="tpu_custom_call" | custom-call | tf_op jit(solution)/shard_map/pallas_call | solution.py:504
  227.2 0.0 copy-start.2
  227.2 2.2 copy.51
  229.5 2.3 copy.50
  231.7 0.0 copy-done.2
  231.7 0.1 convert_multiply_fusion
  231.9 0.0 copy-start
  231.9 1.1 copy-done
  233.0 0.1 slice.47
  233.1 0.6 copy.46
  233.7 2.8 %reshape.58 = f32[3,192,3,192]{3,2,1,0:T(4,128)S(1)} reshape(f32[576,576]{1,0:T(8,128)} %bitcast.32) | data formatting | bytes 2654208 | tf_op jit(solution)/shard_map/reshape | solution.py:556
  236.6 1.2 fusion.5
  237.8 1.8 pad_maximum_fusion
  239.6 1.5 copy.41
  (1 shorter events, 0.0 us)
Async XLA Ops:
  0.6 2.7 %copy-start.3 = (bf16[4,192,2,128]{3,2,1,0:T(2,128)(2,1)S(1)}, bf16[4,192,2,128]{3,2,1,0:T(2,128)(2,1)}, u32[]{:S(2)}) copy-start(bf16[4,192,2,128]{3,2,1,0:T(2,128)(2,1)} %param.4) | copy-start | bytes 1179652
  1.5 3.0 %copy-start.1 = (bf16[1,192,9,192]{3,1,2,0:T(8,128)(2,1)S(1)}, bf16[1,192,9,192]{3,1,2,0:T(8,128)(2,1)}, u32[]{:S(2)}) copy-start(bf16[1,192,9,192]{3,1,2,0:T(8,128)(2,1)} %param.5) | copy-start | bytes 1990660
  227.2 4.5 %copy-start.2 = (bf16[2,6,3,16,640]{4,3,2,1,0:T(8,128)(2,1)S(1)}, bf16[2,6,3,16,640]{4,3,2,1,0:T(8,128)(2,1)}, u32[]{:S(2)}) copy-start(bf16[2,6,3,16,640]{4,3,2,1,0:T(8,128)(2,1)} %get-tuple-element.9) | copy-start | bytes 2211844
  231.9 1.1 copy-start

commit v4 on v3

--- a/solution.py
+++ b/solution.py
@@ -31,15 +31,15 @@
 
 
 def network_kernel(
-    dims, x_ref, w_ref, so_ref, sa_ref, gw_ref,
-    xc, wall, b2, pbuf, gbuf, sbuf, dwf, cr, cs, r2, st2, r3, red, xsem, wss, wrs,
+    dims, normalizer, x_ref, w_ref, b_ref, so_ref, sa_ref, kg_ref, bg_ref,
+    gw_ref, xc, wall, b2, pbuf, gbuf, sbuf, dwf, cr, cs, r2, st2, r3, red, xsem, wss, wrs,
     hss, hrs, oss, ors, crs, crr, r2s, r2r, r3s, r3r, r4s, r4r, r5s, r5r, r6,
 ):
     C, W, nz = dims
     K3 = 3 * C
     half = K3 // 2
     part = half // 2
-    lanes = w_ref.shape[1]
+    lanes = pbuf.shape[1]
     nlat = 2 * nz
     nrow = 4 * nz
     piece = half // PIECES
@@ -122,7 +122,17 @@
         def _():
             pltpu.make_async_copy(xc.at[span], xc.at[span], xsem.at[1, what]).wait()
 
-    wall[seg] = w_ref[...].reshape(2, 2, part, lanes)
+    lane = lax.broadcasted_iota(jnp.int32, (C, lanes - K3), 1)
+    offsets = b_ref[:, 0 : lanes - K3]
+    coarse = offsets.astype(BF).astype(F32)
+    side = jnp.where(lane == 0, coarse, jnp.where(lane == 1, offsets - coarse, 0.0)).astype(BF)
+    table = [
+        jnp.concatenate(
+            [w_ref[q], w_ref[6 + q], w_ref[3 + q], side if q == 1 else jnp.zeros_like(side)], axis=1
+        )
+        for q in range(3)
+    ]
+    wall[seg] = jnp.concatenate(table, axis=0).reshape(2, 2, part, lanes)
     sec_dn, sec_up = x_lo * 4 + y_dn, x_lo * 4 + y_up
     sec_far = x_lo * 4 + lax.rem(y + 2, 4)
     sends = []
@@ -473,6 +483,14 @@
     lax.fori_loop(0, SECTIONS, ended, 0)
     last.wait_send()
     pltpu.make_async_copy(gw_ref.at[other], gw_ref.at[other], r6.at[1]).wait()
+    grads = gw_ref[...].reshape(K3, lanes).astype(F32) * normalizer
+    for q in range(3):
+        block = grads[q * C : (q + 1) * C]
+        kg_ref[q] = block[:, 0:C]
+        kg_ref[6 + q] = block[:, C : 2 * C]
+        kg_ref[3 + q] = block[:, 2 * C : K3]
+        if q == 1:
+            bg_ref[...] = block[:, lanes - 128 :].T[K3 - lanes + 128 : K3 - lanes + 129]
 
 
 def per_device(nz, initial, kernel, bias, cotangent):
@@ -485,32 +503,28 @@
     piece = half // PIECES
     unit = piece // UNITS
 
-    stacked = jnp.concatenate([initial[None], cotangent[1:2], cotangent[0:1]], axis=0)
-    rows = lax.dynamic_slice(
-        stacked, (0, y, 0, 0, 0), (3, 1, C, 2, W)
-    ).reshape(3, C, 2, W).transpose(2, 0, 1, 3)
-
-    taps = kernel[0].reshape(C, 3, 3, C)
-    taps = jnp.concatenate([taps[:, 0:1], taps[:, 2:3], taps[:, 1:2]], axis=1)
-    flat = taps.transpose(2, 0, 1, 3).reshape(K3, K3)
-    coarse = lax.reduce_precision(bias[0], 8, 7)
-    fine = bias[0] - coarse
-    pair = jnp.stack([coarse, fine], axis=1).astype(BF)
-    side = jnp.pad(pair, ((C, C), (0, lanes - K3 - 2)))
-    weights = jnp.concatenate([flat, side], axis=1)
+    normalizer = 1.0 / math.sqrt(initial.shape[0] * 2 * initial.shape[2] * nlat * W)
+    rows = jnp.stack([
+        lax.dynamic_index_in_dim(band, y, 0, keepdims=False)
+        for band in (initial, cotangent[1], cotangent[0])
+    ]).transpose(2, 0, 1, 3)
+    weights = kernel[0].transpose(1, 0, 2)
+    offsets = jnp.broadcast_to(bias[0][:, None], (C, 128))
 
     vm = pl.BlockSpec(memory_space=pltpu.VMEM)
     dma = pltpu.SemaphoreType.DMA
-    so, sa, gw = pl.pallas_call(
-        functools.partial(network_kernel, (C, W, nz)),
+    so, sa, kg, bg = pl.pallas_call(
+        functools.partial(network_kernel, (C, W, nz), normalizer),
         out_shape=(
             jax.ShapeDtypeStruct((8, C, W), BF),
             jax.ShapeDtypeStruct((8, C, W), BF),
-            jax.ShapeDtypeStruct((2, PIECES, UNITS, unit, lanes), BF),
+            jax.ShapeDtypeStruct((9, C, C), F32),
+            jax.ShapeDtypeStruct((1, C), F32),
         ),
-        in_specs=[vm, vm],
-        out_specs=(vm, vm, vm),
+        in_specs=[vm, vm, vm],
+        out_specs=(vm, vm, vm, vm),
         scratch_shapes=[
+            pltpu.VMEM((2, PIECES, UNITS, unit, lanes), BF),
             pltpu.VMEM((3, C, W), BF),
             pltpu.VMEM((SECTIONS, 2, 2, part, lanes), BF),
             pltpu.VMEM((3, K3, C), BF),
@@ -546,20 +560,16 @@
         compiler_params=pltpu.CompilerParams(
             collective_id=0, has_side_effects=True, vmem_limit_bytes=60 * 2**20
         ),
-    )(rows, weights)
+    )(rows, weights, offsets)
 
     def banded(slots):
         return slots.reshape(4, 2, C, W).transpose(0, 2, 1, 3)[None]
 
-    normalizer = 1.0 / math.sqrt(initial.shape[0] * 2 * initial.shape[2] * nlat * W)
-    grads = gw.reshape(K3, lanes).astype(F32) * normalizer
-    core_grads = grads[:, :K3].reshape(3, C, 3, C).transpose(1, 2, 0, 3)
-    core_grads = jnp.concatenate([core_grads[:, 0:1], core_grads[:, 2:3], core_grads[:, 1:2]], axis=1)
     return (
         banded(so),
         banded(sa).astype(F32),
-        core_grads.reshape(1, C, 9, C),
-        grads[C : 2 * C, K3][None],
+        kg.transpose(1, 0, 2)[None],
+        bg,
     )
 
 

time: 241 us -> 227 us (0.942)
  local copies, waits for them, and re-layouts: 16.9 us -> 9.05 us
  other arithmetic: 6.35 us -> 0.75 us
    reshape x2 -> x0, local copies, waits for them, and re-layouts: 3.76 us -> none  [the longest x1 2.82 us: per_device(): core_grads = grads[:, :K3].reshape(3, C, 3, C).transpose(1, 2, 0, 3)]
    concatenate x3 -> x0, other arithmetic: 3.24 us -> none  [the longest x1 1.77 us: per_device(): jnp.concatenate([core_grads[:, 0:1], core_grads[:, 2:3], core_grads[:, 1:...]
where the time goes in v4:
time: 227 us
  Pallas kernels  217 us (96%)
  local copies, waits for them, and re-layouts  9.05 us (4%)
    pallas_call x1, Pallas kernels, per_device(): pl.pallas_call(functools.partial(network_kernel, (C, W, nz), normalizer),...  217 us

profile of v4, /device:TPU:1, one launch (start us, length us, event | category | flops | bytes accessed | tf_op | source)
XLA Modules:
  0.0 227.2 jit_solution(10408197477696034091)
XLA Ops:
  0.6 0.0 copy-start
  0.6 0.0 copy-start.2
  0.7 1.7 fusion
  2.4 0.1 constant_dynamic-slice_fusion
  2.6 0.0 copy-done
  2.6 0.1 constant_dynamic-slice_fusion.2
  2.7 0.7 maximum_bitcast_fusion.x_ref
  3.4 0.0 copy-done.2
  3.4 0.7 broadcast_in_dim.15.b_ref
  4.2 216.7 %shard_map.75 = (bf16[8,192,128]{2,1,0:T(8,128)(2,1)}, bf16[8,192,128]{2,1,0:T(8,128)(2,1)}, f32[9,192,192]{2,1,0:T(8,128)}, f32[1,192]{1,0:T(1,128)}) custom-call(bf16[2,3,192,128]{3,2,1,0:T(8,128)(2,1)} %maximum_bitcast_fusion.x_ref, bf16[9,192,192]{2,1,0:T(8,128)(2,1)} %bitcast.29, f32[192,128]{1,0:T(8,128)} %broadcast_in_dim.15.b_ref), custom_call_target="tpu_custom_call" | custom-call | tf_op jit(solution)/shard_map/pallas_call | solution.py:516
  220.9 0.0 copy-start.1
  220.9 2.4 %copy.18 = f32[4,2,192,128]{3,1,2,0:T(2,128)} copy(bf16[4,2,192,128]{3,2,1,0:T(8,128)(2,1)} %bitcast.35) | data formatting | bytes 1179648 | tf_op jit(solution)/shard_map/convert_element_type | solution.py:570
  223.3 2.1 copy.19
  225.4 0.0 copy-done.1
  225.4 0.0 copy-start.3
  225.4 1.2 copy.24
  226.6 0.0 copy-done.3
  226.6 0.6 copy.25
  (3 shorter events, 0.0 us)
Async XLA Ops:
  0.6 1.9 copy-start
  0.6 2.8 %copy-start.2 = (f32[1,192]{1,0:T(1,128)S(1)}, f32[1,192]{1,0:T(1,128)}, u32[]{:S(2)}) copy-start(f32[1,192]{1,0:T(1,128)} %param.6) | copy-start | bytes 2308
  220.9 4.6 %copy-start.1 = (f32[9,192,192]{2,1,0:T(8,128)S(1)}, f32[9,192,192]{2,1,0:T(8,128)}, u32[]{:S(2)}) copy-start(f32[9,192,192]{2,1,0:T(8,128)} %get-tuple-element.10) | copy-start | bytes 3981316
  225.4 1.2 copy-start.3

commit v5 on v4

--- a/solution.py
+++ b/solution.py
@@ -14,7 +14,7 @@
 BF = jnp.bfloat16
 F32 = jnp.float32
 MESH = pl.DeviceIdType.MESH
-HALO_UP, HALO_DN = 0, 1
+REACH = (1, -1, 2, -2)
 
 
 def silu_value(values):
@@ -66,8 +66,9 @@
         hi = lax.rem(r_band + rz, 2)
         return {"segment": lax.rem(held + hi, 2) * 4 + y, "lat": rz * 2 + hi, "dp": lax.rem(r, 2)}
 
-    up_dev = holder(jnp.maximum(row - 1, 0))
-    dn_dev = holder(jnp.minimum(row + 1, nrow - 1))
+    def inside(shift):
+        return jnp.logical_and(row + shift >= 0, row + shift < nrow)
+
     other = 1 - core
     partner = {"segment": seg, "lat": lat, "dp": other}
     y_up, y_dn = lax.rem(y + 1, 4), lax.rem(y + 3, 4)
@@ -85,42 +86,14 @@
     for d in (1, nz - 1):
         peer = {"segment": seg, "lat": lax.rem(z + d, nz) * 2 + x_hi, "dp": other}
         pl.semaphore_signal(barrier, inc=1, device_id=peer, device_id_type=MESH)
-    pl.semaphore_wait(barrier, 31 + 2 * (nz - 1) + 2)
-
-    def remote(src, dst, ssem, rsem, dev):
-        return pltpu.make_async_remote_copy(
-            src_ref=src, dst_ref=dst, send_sem=ssem, recv_sem=rsem, device_id=dev, device_id_type=MESH
-        )
-
-    giver = core == held
-    stays = jnp.logical_and(giver, odd == 0)
-    home_x = x + odd * (3 - 2 * x)
-
-    def given(r, what):
-        span = pl.ds(0, 1) if what == 0 else pl.ds(1, 2)
-        return remote(
-            x_ref.at[r, span], xc.at[span], xsem.at[0, 2 * r + what], xsem.at[1, what], at(home_x, y, z, r)
-        )
-
-    def leaves(r):
-        return jnp.logical_and(giver, jnp.logical_or(odd == 1, core != r))
-
-    for what in range(2):
-        for r in range(2):
-            @pl.when(leaves(r))
-            def _():
-                given(r, what).start()
-
-    @pl.when(stays)
-    def _():
-        xc[...] = x_ref[core]
-
-    def rows_wait(what):
-        span = pl.ds(0, 1) if what == 0 else pl.ds(1, 2)
-
-        @pl.when(jnp.logical_not(stays))
-        def _():
-            pltpu.make_async_copy(xc.at[span], xc.at[span], xsem.at[1, what]).wait()
+    ones = (lax.broadcasted_iota(jnp.int32, (lanes - K3, W), 0) < 2).astype(F32).astype(BF)
+    for shift in REACH:
+        @pl.when(jnp.logical_not(inside(shift)))
+        def _():
+            @pl.loop(0, APPS // 2)
+            def _(t):
+                sbuf[2 * t, 2 + shift] = jnp.zeros((C, W), BF)
+                gbuf[2 * t + 2, 2 + shift] = jnp.zeros((C, W), BF)
 
     lane = lax.broadcasted_iota(jnp.int32, (C, lanes - K3), 1)
     offsets = b_ref[:, 0 : lanes - K3]
@@ -133,6 +106,43 @@
         for q in range(3)
     ]
     wall[seg] = jnp.concatenate(table, axis=0).reshape(2, 2, part, lanes)
+    pl.semaphore_wait(barrier, 31 + 2 * (nz - 1) + 2)
+
+    def remote(src, dst, ssem, rsem, dev):
+        return pltpu.make_async_remote_copy(
+            src_ref=src, dst_ref=dst, send_sem=ssem, recv_sem=rsem, device_id=dev, device_id_type=MESH
+        )
+
+    giver = core == held
+    stays = jnp.logical_and(giver, odd == 0)
+    home_x = x + odd * (3 - 2 * x)
+
+    def given(r, what):
+        span = pl.ds(0, 1) if what == 0 else pl.ds(1, 2)
+        return remote(
+            x_ref.at[r, span], xc.at[span], xsem.at[0, 2 * r + what], xsem.at[1, what], at(home_x, y, z, r)
+        )
+
+    def leaves(r):
+        return jnp.logical_and(giver, jnp.logical_or(odd == 1, core != r))
+
+    for what in range(2):
+        for r in range(2):
+            @pl.when(leaves(r))
+            def _():
+                given(r, what).start()
+
+    @pl.when(stays)
+    def _():
+        xc[...] = x_ref[core]
+
+    def rows_wait(what):
+        span = pl.ds(0, 1) if what == 0 else pl.ds(1, 2)
+
+        @pl.when(jnp.logical_not(stays))
+        def _():
+            pltpu.make_async_copy(xc.at[span], xc.at[span], xsem.at[1, what]).wait()
+
     sec_dn, sec_up = x_lo * 4 + y_dn, x_lo * 4 + y_up
     sec_far = x_lo * 4 + lax.rem(y + 2, 4)
     sends = []
@@ -146,90 +156,86 @@
 
     dev_yu, dev_yd = at(x, y_up, z), at(x, y_dn, z)
     dev_xu, dev_xd = at(x_up, y, z), at(x_dn, y, z)
-    send_w(0, wall.at[seg, core], 0, dev_yu)
-    send_w(1, wall.at[seg, core], 1, dev_yd)
+    send_w(0, wall.at[seg, core, 0], 0, dev_yu)
+    send_w(1, wall.at[seg, core, 1], 1, dev_yd)
     send_w(2, wall.at[seg, core, 0], 4 + 2 * y, dev_xu)
     send_w(3, wall.at[seg, core, 1], 5 + 2 * y, dev_xd)
+    send_w(19, wall.at[seg, core, 1], 20, dev_yu)
+    send_w(20, wall.at[seg, core, 0], 21, dev_yd)
 
     def landed(ref, slot):
         pltpu.make_async_copy(ref, ref, wrs.at[slot]).wait()
 
-    def spread(index, sec, sy):
-        send_w(index, wall.at[sec, core, 0], 4 + 2 * sy, dev_xu)
-        send_w(index + 1, wall.at[sec, core, 1], 5 + 2 * sy, dev_xd)
-        send_w(index + 2, wall.at[sec, core], 12 + sec, partner)
-
-    landed(wall.at[sec_dn, core], 0)
+    def across(index, sec, part_at):
+        slot = 4 + 2 * lax.rem(sec, 4) + part_at
+        send_w(index, wall.at[sec, core, part_at], slot, dev_xu if part_at == 0 else dev_xd)
+
+    def beside(index, sec):
+        send_w(index, wall.at[sec, core], 12 + sec, partner)
+
+    landed(wall.at[sec_dn, core, 0], 0)
     send_w(4, wall.at[sec_dn, core, 0], 2, dev_yu)
-    spread(5, sec_dn, y_dn)
-    landed(wall.at[sec_up, core], 1)
+    across(5, sec_dn, 0)
+    landed(wall.at[sec_up, core, 1], 1)
     send_w(8, wall.at[sec_up, core, 1], 3, dev_yd)
-    spread(9, sec_up, y_up)
+    across(10, sec_up, 1)
+    landed(wall.at[sec_dn, core, 1], 20)
+    across(6, sec_dn, 1)
+    beside(7, sec_dn)
+    landed(wall.at[sec_up, core, 0], 21)
+    across(9, sec_up, 0)
+    beside(11, sec_up)
     landed(wall.at[sec_far, core, 0], 2)
+    across(12, sec_far, 0)
     landed(wall.at[sec_far, core, 1], 3)
-    spread(12, sec_far, lax.rem(y + 2, 4))
-    for j in range(4):
-        sy = lax.rem(y + j, 4)
-        sec = (1 - x_lo) * 4 + sy
-        landed(wall.at[sec, core, 0], 4 + 2 * sy)
-        landed(wall.at[sec, core, 1], 5 + 2 * sy)
-        send_w(15 + j, wall.at[sec, core], 12 + sec, partner)
-    for j in range(1, 8):
-        sec = lax.rem(seg + j, 8)
-        landed(wall.at[sec, other], 12 + sec)
-
-    ones = (lax.broadcasted_iota(jnp.int32, (lanes - K3, W), 0) < 2).astype(F32).astype(BF)
-
-    @pl.loop(0, APPS)
-    def _(a):
-        pbuf[a, K3:, :] = ones
-
-    @pl.when(jnp.logical_not(has_up))
-    def _():
-        @pl.loop(0, APPS)
-        def _(a):
-            pbuf[a, 0:C, :] = jnp.zeros((C, W), BF)
-            gbuf[a + 1, 0:C, :] = jnp.zeros((C, W), BF)
-
-    @pl.when(jnp.logical_not(has_dn))
-    def _():
-        @pl.loop(0, APPS)
-        def _(a):
-            pbuf[a, C : 2 * C, :] = jnp.zeros((C, W), BF)
-            gbuf[a + 1, C : 2 * C, :] = jnp.zeros((C, W), BF)
-
+    across(13, sec_far, 1)
+    beside(14, sec_far)
+
+    def beside_copy(sec):
+        half_ref = wall.at[sec, core]
+        return remote(half_ref, half_ref, wss.at[15 + lax.rem(sec, 4)], wrs.at[12 + sec], partner)
+
+    def take_section(sec):
+        @pl.when(jnp.logical_and(sec < SECTIONS, sec // 4 != x_lo))
+        def _():
+            sy = lax.rem(sec, 4)
+            landed(wall.at[sec, core, 0], 4 + 2 * sy)
+            landed(wall.at[sec, core, 1], 5 + 2 * sy)
+            beside_copy(sec).start()
+
+    def need_section(sec):
+        @pl.when(jnp.logical_and(sec < SECTIONS, sec != seg))
+        def _():
+            landed(wall.at[sec, other], 12 + sec)
+
+    take_section(jnp.int32(0))
+    take_section(jnp.int32(1))
     rows_wait(0)
-    sbuf[0] = xc[0]
-
-    def halo_copies(buf, slot, step):
-        own = buf.at[slot, pl.ds(2 * C, C), :]
-        to_up = remote(own, buf.at[slot, pl.ds(C, C), :], hss.at[step, 0], hrs.at[step, 1], up_dev)
-        to_dn = remote(own, buf.at[slot, pl.ds(0, C), :], hss.at[step, 1], hrs.at[step, 0], dn_dev)
-        return to_up, to_dn
+    sbuf[0, 2] = xc[0]
+
+    def halo_copy(buf, slot, step, shift):
+        return remote(
+            buf.at[slot, 2], buf.at[slot, 2 - shift], hss.at[step, 2 + shift], hrs.at[step, 2 - shift],
+            holder(jnp.clip(row + shift, 0, nrow - 1)),
+        )
 
     def halo_start(buf, slot, step):
-        to_up, to_dn = halo_copies(buf, slot, step)
-
-        @pl.when(has_up)
-        def _():
-            to_up.start()
-
-        @pl.when(has_dn)
-        def _():
-            to_dn.start()
+        for shift in REACH:
+            @pl.when(inside(shift))
+            def _():
+                halo_copy(buf, slot, step, shift).start()
 
     def halo_wait(buf, slot, step):
-        to_up, to_dn = halo_copies(buf, slot, step)
-
-        @pl.when(has_up)
-        def _():
-            to_up.wait_send()
-            pltpu.make_async_copy(buf.at[slot, pl.ds(0, C), :], buf.at[slot, pl.ds(0, C), :], hrs.at[step, 0]).wait()
-
-        @pl.when(has_dn)
-        def _():
-            to_dn.wait_send()
-            pltpu.make_async_copy(buf.at[slot, pl.ds(C, C), :], buf.at[slot, pl.ds(C, C), :], hrs.at[step, 1]).wait()
+        for shift in REACH:
+            @pl.when(inside(shift))
+            def _():
+                there = buf.at[slot, 2 + shift]
+                pltpu.make_async_copy(there, there, hrs.at[step, 2 + shift]).wait()
+
+        for shift in REACH:
+            @pl.when(inside(shift))
+            def _():
+                halo_copy(buf, slot, step, shift).wait_send()
 
     out_slot = y * 2 + core
 
@@ -255,38 +261,69 @@
         minus, same, plus = parts[0:C], parts[C : 2 * C], parts[2 * C :]
         return same + pltpu.roll(minus, 1 if sign < 0 else W - 1, 1) + pltpu.roll(plus, W - 1 if sign < 0 else 1, 1)
 
-    def forward(a, carry):
+    def kept(shift, values):
+        return jnp.where(inside(shift), values, jnp.zeros_like(values))
+
+    def beside_each_other(*blocks):
+        return jnp.concatenate(blocks, axis=1)
+
+    def activated(state):
+        return silu_value(state.astype(F32)).astype(BF)
+
+    def state_out(number):
+        @pl.when(number > APPS - SECTIONS)
+        def _():
+            out_send(sbuf.at[number, 2], so_ref, 0, number - 1 - (APPS - SECTIONS))
+
+    def forward(t, carry):
+        a = 2 * t
+        halo_start(sbuf, a, t)
+        take_section(a + 2)
+        take_section(a + 3)
+        state_out(a - 1)
+        state_out(a)
+        need_section(a)
+        need_section(a + 1)
         k = lax.rem(a, SECTIONS)
-        state = sbuf[a].astype(F32)
-        pbuf[a, 2 * C : K3, :] = silu_value(state).astype(BF)
-        halo_start(pbuf, a, a)
-        own = jnp.dot(
-            wall[k, :, :, :, 2 * C :].reshape(K3, lanes - 2 * C), pbuf[a, 2 * C :, :], preferred_element_type=F32
-        )
-        halo_wait(pbuf, a, a)
-        rest = jnp.dot(
-            wall[k, :, :, :, 0 : 2 * C].reshape(K3, 2 * C), pbuf[a, 0 : 2 * C, :], preferred_element_type=F32
-        )
-        sbuf[a + 1] = (state + shifted_sum(own + rest, -1)).astype(BF)
-
-        @pl.when(a >= APPS - SECTIONS)
-        def _():
-            out_send(sbuf.at[a + 1], so_ref, 0, k)
-
+        table = wall[k].reshape(K3, lanes)
+        halo_wait(sbuf, a, t)
+        acts = [activated(sbuf[a, i]) for i in range(5)]
+        pbuf[a] = jnp.concatenate([acts[1], acts[3], acts[2], ones], axis=0)
+        wide = jnp.concatenate(
+            [
+                beside_each_other(acts[0], acts[1], acts[2]),
+                beside_each_other(acts[2], acts[3], acts[4]),
+                beside_each_other(acts[1], acts[2], acts[3]),
+                beside_each_other(ones, ones, ones),
+            ],
+            axis=0,
+        )
+        sums = jnp.dot(table, wide, preferred_element_type=F32)
+        nexts = []
+        for m in range(3):
+            branch = shifted_sum(sums[:, m * W : (m + 1) * W], -1)
+            value = kept(m - 1, (sbuf[a, 1 + m].astype(F32) + branch).astype(BF))
+            sbuf[a + 1, 1 + m] = value
+            nexts.append(value)
+        acts = [activated(value) for value in nexts]
+        column = jnp.concatenate([acts[0], acts[2], acts[1], ones], axis=0)
+        pbuf[a + 1] = column
+        sums = jnp.dot(wall[lax.rem(a + 1, SECTIONS)].reshape(K3, lanes), column, preferred_element_type=F32)
+        sbuf[a + 2, 2] = (nexts[1].astype(F32) + shifted_sum(sums, -1)).astype(BF)
         return carry
 
-    lax.fori_loop(0, APPS, forward, 0)
+    lax.fori_loop(0, APPS // 2, forward, 0)
 
     rows_wait(1)
-    gbuf[APPS, 2 * C :, :] = xc[1]
-
-    def turned_weights(k):
+    gbuf[APPS, 2] = xc[1]
+
+    def turned_weights(k, which):
+        table = wall[k].reshape(K3, lanes)
         for q in range(3):
-            flat = wall[k].reshape(K3, lanes)[q * C : (q + 1) * C]
-            turned = flat[:, : K3].T
-            b2[1, q * C : (q + 1) * C, :] = turned[0:C]
-            b2[0, q * C : (q + 1) * C, :] = turned[C : 2 * C]
-            b2[2, q * C : (q + 1) * C, :] = turned[2 * C :]
+            turned = table[q * C : (q + 1) * C, :K3].T
+            b2[which, 1, q * C : (q + 1) * C, :] = turned[0:C]
+            b2[which, 0, q * C : (q + 1) * C, :] = turned[C : 2 * C]
+            b2[which, 2, q * C : (q + 1) * C, :] = turned[2 * C :]
 
     def tapped(grad):
         wide = grad.astype(F32)
@@ -371,58 +408,92 @@
                 remote(red.at[k], gw_ref.at[core, my_piece], r5s.at[k], r5r.at[my_piece], dev).start()
 
     def staged(a):
-        for lag, stage in ((1, pair_and_scatter), (3, sum_and_scatter), (5, lat_sum), (7, deliver)):
+        for lag, stage in ((2, pair_and_scatter), (4, sum_and_scatter), (6, lat_sum), (8, deliver)):
             k = a + lag
 
             @pl.when(jnp.logical_and(k >= 0, k < SECTIONS))
             def _():
                 stage(k)
 
-    def backward(a, with_weights):
-        k = lax.rem(a, SECTIONS)
-        step = APPS + APPS - 1 - a
-        slot = a + 1
-        halo_start(gbuf, slot, step)
-        grad = gbuf[slot, 2 * C :, :]
-        turned_weights(k)
-        own = jnp.dot(b2[2], grad, preferred_element_type=F32)
+    def weight_work(k):
+        later = k + SECTIONS
+        taps = jnp.concatenate([tapped(gbuf[k + 1, 2]), tapped(gbuf[later + 1, 2])], axis=1)
+        acts = jnp.concatenate([pbuf[k], pbuf[later]], axis=1)
+        dw = lax.dot_general(taps, acts, (((1,), (1,)), ((), ())), preferred_element_type=F32)
+        dwf[k] = dw.astype(BF).reshape(2, PIECES, piece, lanes)
+        remote(dwf.at[k, other], cr.at[k], crs.at[k], crr.at[k], partner).start()
+        staged(k)
+
+    def adjoint_out(k):
+        @pl.when(k < SECTIONS)
+        def _():
+            out_send(gbuf.at[k, 2], sa_ref, 1, k)
+
+    def backward(t, with_weights):
+        b = 2 * t + 1
+        a = 2 * t
+        step = APPS - 1 - t
+        halo_start(gbuf, b + 1, step)
         if with_weights:
-            later = a + SECTIONS
-            taps = jnp.concatenate([tapped(grad), tapped(gbuf[later + 1, 2 * C :, :])], axis=1)
-            acts = jnp.concatenate([pbuf[a], pbuf[later]], axis=1)
-            dw = lax.dot_general(taps, acts, (((1,), (1,)), ((), ())), preferred_element_type=F32)
-            dwf[k] = dw.astype(BF).reshape(2, PIECES, piece, lanes)
-            remote(dwf.at[k, other], cr.at[k], crs.at[k], crr.at[k], partner).start()
-            staged(a)
-
-        halo_wait(gbuf, slot, step)
-        rest = jnp.dot(b2[0], gbuf[slot, 0:C, :], preferred_element_type=F32) + jnp.dot(
-            b2[1], gbuf[slot, C : 2 * C, :], preferred_element_type=F32
-        )
-        slope = silu_slope(sbuf[a].astype(F32))
-        adjoint = grad.astype(F32) + slope * shifted_sum(own + rest, 1)
+            adjoint_out(b + 2)
+            adjoint_out(b + 1)
+        else:
+            @pl.when(b == APPS - 1)
+            def _():
+                state_out(jnp.int32(APPS - 1))
+                state_out(jnp.int32(APPS))
+        turned_weights(lax.rem(b, SECTIONS), 0)
+        turned_weights(lax.rem(a, SECTIONS), 1)
+        if with_weights:
+            @pl.when(b < SECTIONS - 1)
+            def _():
+                weight_work(b + 1)
+
+            weight_work(b)
+        halo_wait(gbuf, b + 1, step)
+        g = [gbuf[b + 1, i] for i in range(5)]
+        sums = (
+            jnp.dot(b2[0, 2], beside_each_other(g[1], g[2], g[3]), preferred_element_type=F32)
+            + jnp.dot(b2[0, 0], beside_each_other(g[0], g[1], g[2]), preferred_element_type=F32)
+            + jnp.dot(b2[0, 1], beside_each_other(g[2], g[3], g[4]), preferred_element_type=F32)
+        )
+        grads = []
+        for m in range(3):
+            moved = shifted_sum(sums[:, m * W : (m + 1) * W], 1)
+            slope = silu_slope(sbuf[b, 1 + m].astype(F32))
+            value = kept(m - 1, (g[1 + m].astype(F32) + slope * moved).astype(BF))
+            gbuf[b, 1 + m] = value
+            grads.append(value)
+        sums = (
+            jnp.dot(b2[1, 2], grads[1], preferred_element_type=F32)
+            + jnp.dot(b2[1, 0], grads[0], preferred_element_type=F32)
+            + jnp.dot(b2[1, 1], grads[2], preferred_element_type=F32)
+        )
+        slope = silu_slope(sbuf[a, 2].astype(F32))
+        adjoint = grads[1].astype(F32) + slope * shifted_sum(sums, 1)
         if not with_weights:
             adjoint = adjoint + jnp.where(a == SECTIONS, xc[2].astype(F32), 0.0)
-        gbuf[a, 2 * C :, :] = adjoint.astype(BF)
-        if with_weights:
-            out_send(gbuf.at[a, pl.ds(2 * C, C), :], sa_ref, 1, k)
+        gbuf[a, 2] = adjoint.astype(BF)
 
     def backward_late(i, carry):
-        backward(APPS - 1 - i, False)
+        backward(APPS // 2 - 1 - i, False)
         return carry
 
     def backward_early(i, carry):
-        backward(SECTIONS - 1 - i, True)
+        backward(SECTIONS // 2 - 1 - i, True)
         return carry
 
-    lax.fori_loop(0, SECTIONS, backward_late, 0)
-    lax.fori_loop(0, SECTIONS, backward_early, 0)
+    lax.fori_loop(0, (APPS - SECTIONS) // 2, backward_late, 0)
+    lax.fori_loop(0, SECTIONS // 2, backward_early, 0)
+    weight_work(jnp.int32(0))
+    adjoint_out(jnp.int32(1))
+    adjoint_out(jnp.int32(0))
 
     def drain(i, carry):
         staged(-1 - i)
         return carry
 
-    lax.fori_loop(0, 7, drain, 0)
+    lax.fori_loop(0, 8, drain, 0)
     for j in range(PIECES):
         @pl.when(seg != (j // 3) * 4 + j % 3)
         def _():
@@ -432,9 +503,11 @@
 
     for copy in sends:
         copy.wait_send()
+    for j in range(4):
+        beside_copy((1 - x_lo) * 4 + j).wait_send()
     for k in range(SECTIONS):
         for which, (dst, src) in enumerate(
-            ((so_ref, sbuf.at[APPS - SECTIONS + k + 1]), (sa_ref, gbuf.at[k, pl.ds(2 * C, C), :]))
+            ((so_ref, sbuf.at[APPS - SECTIONS + k + 1, 2]), (sa_ref, gbuf.at[k, 2]))
         ):
             @pl.when(jnp.logical_not(is_self(k)))
             def _():
@@ -527,10 +600,10 @@
             pltpu.VMEM((2, PIECES, UNITS, unit, lanes), BF),
             pltpu.VMEM((3, C, W), BF),
             pltpu.VMEM((SECTIONS, 2, 2, part, lanes), BF),
-            pltpu.VMEM((3, K3, C), BF),
+            pltpu.VMEM((2, 3, K3, C), BF),
             pltpu.VMEM((APPS, lanes, W), BF),
-            pltpu.VMEM((APPS + 1, K3, W), BF),
-            pltpu.VMEM((APPS + 1, C, W), BF),
+            pltpu.VMEM((APPS + 1, 5, C, W), BF),
+            pltpu.VMEM((APPS + 1, 5, C, W), BF),
             pltpu.VMEM((SECTIONS, 2, PIECES, piece, lanes), BF),
             pltpu.VMEM((SECTIONS, PIECES, piece, lanes), BF),
             pltpu.VMEM((SECTIONS, PIECES, piece, lanes), BF),
@@ -539,10 +612,10 @@
             pltpu.VMEM((SECTIONS, nlat, unit, lanes), BF),
             pltpu.VMEM((SECTIONS, UNITS, unit, lanes), BF),
             dma((2, 4)),
-            dma((19,)),
-            dma((20,)),
-            dma((2 * APPS, 2)),
-            dma((2 * APPS, 2)),
+            dma((21,)),
+            dma((22,)),
+            dma((APPS, 5)),
+            dma((APPS, 5)),
             dma((2, SECTIONS)),
             dma((2, 8)),
             dma((SECTIONS,)),

time: 227 us -> 204 us (0.90)
  Pallas kernels: 217 us -> 193 us
    pallas_call x1, Pallas kernels: 217 us -> 193 us  [per_device(): pl.pallas_call(functools.partial(network_kernel, (C, W, nz), normalizer),...]
where the time goes in v5:
time: 204 us; the launch traced here: 203 us
  Pallas kernels  193 us (95%)
  local copies, waits for them, and re-layouts  9.05 us (4%)
    pallas_call x1, Pallas kernels, per_device(): pl.pallas_call(functools.partial(network_kernel, (C, W, nz), normalizer),...  193 us

profile of v5, /device:TPU:1, one launch (start us, length us, event | category | flops | bytes accessed | tf_op | source)
XLA Modules:
  0.0 203.4 jit_solution(15318109991209030320)
XLA Ops:
  0.6 0.0 copy-start
  0.6 0.0 copy-start.2
  0.7 1.7 fusion
  2.4 0.1 constant_dynamic-slice_fusion
  2.6 0.0 copy-done
  2.6 0.1 constant_dynamic-slice_fusion.2
  2.7 0.7 maximum_bitcast_fusion.x_ref
  3.4 0.0 copy-done.2
  3.4 0.7 broadcast_in_dim.15.b_ref
  4.2 192.8 %shard_map.75 = (bf16[8,192,128]{2,1,0:T(8,128)(2,1)}, bf16[8,192,128]{2,1,0:T(8,128)(2,1)}, f32[9,192,192]{2,1,0:T(8,128)}, f32[1,192]{1,0:T(1,128)}) custom-call(bf16[2,3,192,128]{3,2,1,0:T(8,128)(2,1)} %maximum_bitcast_fusion.x_ref, bf16[9,192,192]{2,1,0:T(8,128)(2,1)} %bitcast.29, f32[192,128]{1,0:T(8,128)} %broadcast_in_dim.15.b_ref), custom_call_target="tpu_custom_call" | custom-call | tf_op jit(solution)/shard_map/pallas_call | solution.py:589
  197.0 0.0 copy-start.1
  197.0 2.4 %copy.18 = f32[4,2,192,128]{3,1,2,0:T(2,128)} copy(bf16[4,2,192,128]{3,2,1,0:T(8,128)(2,1)} %bitcast.35) | data formatting | bytes 1179648 | tf_op jit(solution)/shard_map/convert_element_type | solution.py:643
  199.4 2.1 %copy.19 = bf16[4,2,192,128]{3,1,2,0:T(2,128)(2,1)} copy(bf16[4,2,192,128]{3,2,1,0:T(8,128)(2,1)} %bitcast.32) | data formatting | bytes 786432 | tf_op jit(solution)/shard_map/reshape | solution.py:639
  201.6 0.0 copy-done.1
  201.6 0.0 copy-start.3
  201.6 1.2 copy.24
  202.8 0.0 copy-done.3
  202.8 0.6 copy.25
  (3 shorter events, 0.0 us)
Async XLA Ops:
  0.6 1.9 copy-start
  0.6 2.8 %copy-start.2 = (f32[1,192]{1,0:T(1,128)S(1)}, f32[1,192]{1,0:T(1,128)}, u32[]{:S(2)}) copy-start(f32[1,192]{1,0:T(1,128)} %param.6) | copy-start | bytes 2308
  197.0 4.6 %copy-start.1 = (f32[9,192,192]{2,1,0:T(8,128)S(1)}, f32[9,192,192]{2,1,0:T(8,128)}, u32[]{:S(2)}) copy-start(f32[9,192,192]{2,1,0:T(8,128)} %get-tuple-element.10) | copy-start | bytes 3981316
  201.6 1.2 copy-start.3

commit v6 on v5

--- a/solution.py
+++ b/solution.py
@@ -165,6 +165,34 @@
 
     def landed(ref, slot):
         pltpu.make_async_copy(ref, ref, wrs.at[slot]).wait()
+
+    def halo_copy(buf, slot, step, shift):
+        return remote(
+            buf.at[slot, 2], buf.at[slot, 2 - shift], hss.at[step, 2 + shift], hrs.at[step, 2 - shift],
+            holder(jnp.clip(row + shift, 0, nrow - 1)),
+        )
+
+    def halo_start(buf, slot, step):
+        for shift in REACH:
+            @pl.when(inside(shift))
+            def _():
+                halo_copy(buf, slot, step, shift).start()
+
+    def halo_wait(buf, slot, step):
+        for shift in REACH:
+            @pl.when(inside(shift))
+            def _():
+                there = buf.at[slot, 2 + shift]
+                pltpu.make_async_copy(there, there, hrs.at[step, 2 + shift]).wait()
+
+        for shift in REACH:
+            @pl.when(inside(shift))
+            def _():
+                halo_copy(buf, slot, step, shift).wait_send()
+
+    rows_wait(0)
+    sbuf[0, 2] = xc[0]
+    halo_start(sbuf, 0, 0)
 
     def across(index, sec, part_at):
         slot = 4 + 2 * lax.rem(sec, 4) + part_at
@@ -210,33 +238,6 @@
 
     take_section(jnp.int32(0))
     take_section(jnp.int32(1))
-    rows_wait(0)
-    sbuf[0, 2] = xc[0]
-
-    def halo_copy(buf, slot, step, shift):
-        return remote(
-            buf.at[slot, 2], buf.at[slot, 2 - shift], hss.at[step, 2 + shift], hrs.at[step, 2 - shift],
-            holder(jnp.clip(row + shift, 0, nrow - 1)),
-        )
-
-    def halo_start(buf, slot, step):
-        for shift in REACH:
-            @pl.when(inside(shift))
-            def _():
-                halo_copy(buf, slot, step, shift).start()
-
-    def halo_wait(buf, slot, step):
-        for shift in REACH:
-            @pl.when(inside(shift))
-            def _():
-                there = buf.at[slot, 2 + shift]
-                pltpu.make_async_copy(there, there, hrs.at[step, 2 + shift]).wait()
-
-        for shift in REACH:
-            @pl.when(inside(shift))
-            def _():
-                halo_copy(buf, slot, step, shift).wait_send()
-
     out_slot = y * 2 + core
 
     def out_copy(src, dst, which, k):
@@ -277,7 +278,11 @@
 
     def forward(t, carry):
         a = 2 * t
-        halo_start(sbuf, a, t)
+
+        @pl.when(t > 0)
+        def _():
+            halo_start(sbuf, a, t)
+
         take_section(a + 2)
         take_section(a + 3)
         state_out(a - 1)
@@ -338,7 +343,7 @@
                 j = 3 * jx + jy
                 cs[k, j] = (dwf[k, core, j].astype(F32) + cr[k, j].astype(F32)).astype(BF)
                 near = x_lo == jx
-                far_x = lax.rem(x + (1 if jy % 2 == 0 else 3), 4)
+                far_x = x + 1 - 2 * x_lo
                 home = at(jnp.where(near, x, far_x), jy, z)
                 slot = jnp.where(near, y, 4 + y)
                 mine = jnp.logical_and(near, y == jy)
@@ -407,8 +412,8 @@
                 dev = {"segment": k, "lat": lat, "dp": core}
                 remote(red.at[k], gw_ref.at[core, my_piece], r5s.at[k], r5r.at[my_piece], dev).start()
 
-    def staged(a):
-        for lag, stage in ((2, pair_and_scatter), (4, sum_and_scatter), (6, lat_sum), (8, deliver)):
+    def staged(a, first=0):
+        for lag, stage in ((1, pair_and_scatter), (4, sum_and_scatter), (6, lat_sum), (8, deliver))[first:]:
             k = a + lag
 
             @pl.when(jnp.logical_and(k >= 0, k < SECTIONS))
@@ -422,7 +427,6 @@
         dw = lax.dot_general(taps, acts, (((1,), (1,)), ((), ())), preferred_element_type=F32)
         dwf[k] = dw.astype(BF).reshape(2, PIECES, piece, lanes)
         remote(dwf.at[k, other], cr.at[k], crs.at[k], crr.at[k], partner).start()
-        staged(k)
 
     def adjoint_out(k):
         @pl.when(k < SECTIONS)
@@ -448,8 +452,10 @@
             @pl.when(b < SECTIONS - 1)
             def _():
                 weight_work(b + 1)
+                staged(b + 1)
 
             weight_work(b)
+            staged(b)
         halo_wait(gbuf, b + 1, step)
         g = [gbuf[b + 1, i] for i in range(5)]
         sums = (
@@ -486,11 +492,14 @@
     lax.fori_loop(0, (APPS - SECTIONS) // 2, backward_late, 0)
     lax.fori_loop(0, SECTIONS // 2, backward_early, 0)
     weight_work(jnp.int32(0))
+    pair_and_scatter(jnp.int32(1))
+    pair_and_scatter(jnp.int32(0))
     adjoint_out(jnp.int32(1))
     adjoint_out(jnp.int32(0))
+    staged(jnp.int32(0), 1)
 
     def drain(i, carry):
-        staged(-1 - i)
+        staged(-1 - i, 1)
         return carry
 
     lax.fori_loop(0, 8, drain, 0)

time: 204 us -> 211 us (1.034)
  Pallas kernels: 193 us -> 200 us
    pallas_call x1, Pallas kernels: 193 us -> 200 us  [per_device(): pl.pallas_call(functools.partial(network_kernel, (C, W, nz), normalizer),...]
where the time goes in v6:
time: 211 us
  Pallas kernels  200 us (95%)
  local copies, waits for them, and re-layouts  9.05 us (4%)
    pallas_call x1, Pallas kernels, per_device(): pl.pallas_call(functools.partial(network_kernel, (C, W, nz), normalizer),...  200 us

profile of v6, /device:TPU:1, one launch (start us, length us, event | category | flops | bytes accessed | tf_op | source)
XLA Modules:
  0.0 210.7 jit_solution(6405629856647187089)
XLA Ops:
  0.6 0.0 copy-start
  0.6 0.0 copy-start.2
  0.7 1.7 fusion
  2.4 0.1 constant_dynamic-slice_fusion
  2.6 0.0 copy-done
  2.6 0.1 constant_dynamic-slice_fusion.2
  2.7 0.7 maximum_bitcast_fusion.x_ref
  3.4 0.0 copy-done.2
  3.4 0.7 broadcast_in_dim.15.b_ref
  4.2 200.1 %shard_map.75 = (bf16[8,192,128]{2,1,0:T(8,128)(2,1)}, bf16[8,192,128]{2,1,0:T(8,128)(2,1)}, f32[9,192,192]{2,1,0:T(8,128)}, f32[1,192]{1,0:T(1,128)}) custom-call(bf16[2,3,192,128]{3,2,1,0:T(8,128)(2,1)} %maximum_bitcast_fusion.x_ref, bf16[9,192,192]{2,1,0:T(8,128)(2,1)} %bitcast.29, f32[192,128]{1,0:T(8,128)} %broadcast_in_dim.15.b_ref), custom_call_target="tpu_custom_call" | custom-call | tf_op jit(solution)/shard_map/pallas_call | solution.py:598
  204.3 0.0 copy-start.1
  204.3 2.4 %copy.18 = f32[4,2,192,128]{3,1,2,0:T(2,128)} copy(bf16[4,2,192,128]{3,2,1,0:T(8,128)(2,1)} %bitcast.35) | data formatting | bytes 1179648 | tf_op jit(solution)/shard_map/convert_element_type | solution.py:652
  206.8 2.1 %copy.19 = bf16[4,2,192,128]{3,1,2,0:T(2,128)(2,1)} copy(bf16[4,2,192,128]{3,2,1,0:T(8,128)(2,1)} %bitcast.32) | data formatting | bytes 786432 | tf_op jit(solution)/shard_map/reshape | solution.py:648
  208.9 0.0 copy-done.1
  208.9 0.0 copy-start.3
  208.9 1.2 copy.24
  210.1 0.0 copy-done.3
  210.1 0.6 copy.25
  (3 shorter events, 0.0 us)
Async XLA Ops:
  0.6 1.9 copy-start
  0.6 2.8 %copy-start.2 = (f32[1,192]{1,0:T(1,128)S(1)}, f32[1,192]{1,0:T(1,128)}, u32[]{:S(2)}) copy-start(f32[1,192]{1,0:T(1,128)} %param.6) | copy-start | bytes 2308
  204.3 4.6 %copy-start.1 = (f32[9,192,192]{2,1,0:T(8,128)S(1)}, f32[9,192,192]{2,1,0:T(8,128)}, u32[]{:S(2)}) copy-start(f32[9,192,192]{2,1,0:T(8,128)} %get-tuple-element.10) | copy-start | bytes 3981316
  208.9 1.2 copy-start.3

commit v7 on v6

--- a/solution.py
+++ b/solution.py
@@ -343,7 +343,7 @@
                 j = 3 * jx + jy
                 cs[k, j] = (dwf[k, core, j].astype(F32) + cr[k, j].astype(F32)).astype(BF)
                 near = x_lo == jx
-                far_x = x + 1 - 2 * x_lo
+                far_x = lax.rem(x + (1 if jy % 2 == 0 else 3), 4)
                 home = at(jnp.where(near, x, far_x), jy, z)
                 slot = jnp.where(near, y, 4 + y)
                 mine = jnp.logical_and(near, y == jy)

time: 211 us -> 201 us (0.953)
  Pallas kernels: 200 us -> 190 us
    pallas_call x1, Pallas kernels: 200 us -> 190 us  [per_device(): pl.pallas_call(functools.partial(network_kernel, (C, W, nz), normalizer),...]
where the time goes in v7:
time: 201 us
  Pallas kernels  190 us (95%)
  local copies, waits for them, and re-layouts  9.05 us (5%)
    pallas_call x1, Pallas kernels, per_device(): pl.pallas_call(functools.partial(network_kernel, (C, W, nz), normalizer),...  190 us

profile of v7, /device:TPU:1, one launch (start us, length us, event | category | flops | bytes accessed | tf_op | source)
XLA Modules:
  0.0 200.6 jit_solution(17646777703164882670)
XLA Ops:
  0.6 0.0 copy-start
  0.6 0.0 copy-start.2
  0.7 1.7 fusion
  2.4 0.1 constant_dynamic-slice_fusion
  2.6 0.0 copy-done
  2.6 0.1 constant_dynamic-slice_fusion.2
  2.7 0.7 maximum_bitcast_fusion.x_ref
  3.4 0.0 copy-done.2
  3.4 0.7 broadcast_in_dim.15.b_ref
  4.2 190.1 %shard_map.75 = (bf16[8,192,128]{2,1,0:T(8,128)(2,1)}, bf16[8,192,128]{2,1,0:T(8,128)(2,1)}, f32[9,192,192]{2,1,0:T(8,128)}, f32[1,192]{1,0:T(1,128)}) custom-call(bf16[2,3,192,128]{3,2,1,0:T(8,128)(2,1)} %maximum_bitcast_fusion.x_ref, bf16[9,192,192]{2,1,0:T(8,128)(2,1)} %bitcast.29, f32[192,128]{1,0:T(8,128)} %broadcast_in_dim.15.b_ref), custom_call_target="tpu_custom_call" | custom-call | tf_op jit(solution)/shard_map/pallas_call | solution.py:598
  194.3 0.0 copy-start.1
  194.3 2.4 %copy.18 = f32[4,2,192,128]{3,1,2,0:T(2,128)} copy(bf16[4,2,192,128]{3,2,1,0:T(8,128)(2,1)} %bitcast.35) | data formatting | bytes 1179648 | tf_op jit(solution)/shard_map/convert_element_type | solution.py:652
  196.7 2.1 %copy.19 = bf16[4,2,192,128]{3,1,2,0:T(2,128)(2,1)} copy(bf16[4,2,192,128]{3,2,1,0:T(8,128)(2,1)} %bitcast.32) | data formatting | bytes 786432 | tf_op jit(solution)/shard_map/reshape | solution.py:648
  198.8 0.0 copy-done.1
  198.8 0.0 copy-start.3
  198.8 1.2 copy.24
  200.0 0.0 copy-done.3
  200.0 0.6 copy.25
  (3 shorter events, 0.0 us)
Async XLA Ops:
  0.6 1.9 copy-start
  0.6 2.8 %copy-start.2 = (f32[1,192]{1,0:T(1,128)S(1)}, f32[1,192]{1,0:T(1,128)}, u32[]{:S(2)}) copy-start(f32[1,192]{1,0:T(1,128)} %param.6) | copy-start | bytes 2308
  194.3 4.6 %copy-start.1 = (f32[9,192,192]{2,1,0:T(8,128)S(1)}, f32[9,192,192]{2,1,0:T(8,128)}, u32[]{:S(2)}) copy-start(f32[9,192,192]{2,1,0:T(8,128)} %get-tuple-element.10) | copy-start | bytes 3981316
  198.8 1.2 copy-start.3
